TPU v7x, 256 devices: a whole 4x4x8 slice. The times are simulated.
256 devices in a mesh: row: 16 (over y_hi, x, core), col: 16 (over y_lo, z).
Axes of the slice: x: 4, y: 4 (y_hi: 2, y_lo: 2; y = y_hi * 2 + y_lo), z: 8, core: 2. Of those that a mesh axis runs over, the one named last changes fastest.
Arguments:
- op_tiles: float32 [512, 16, 64, 64], P('row', 'col'), may hold values from -18 to 18
- op_rows: int32 [512, 16], P('row', 'col'), may hold values from 0 to 7
- op_cols: int32 [512, 16], P('row', 'col'), may hold values from 0 to 7
- op_count: int32 [16, 16], P('row', 'col'), may hold values from 1 to 32, as said below
- pro_tiles: float32 [128, 16, 64, 64], P('row', 'col'), may hold values from -0.125 to 0.125
- pro_cols: int32 [128, 16], P('row', 'col'), may hold values from 0 to 1
- pro_live: int32 [128, 16], P('row', 'col'), may hold values 0 or 1
Outputs:
- product: float32 [128, 32, 64, 64], P('row', 'col')
- coarse: float32 [32, 32, 64, 64], P('row', 'col')
Inputs may be any that keep to these rules, and one draw needn't show every extreme that they name: `op_count`: live slots of each device's list; some device's list is full in every draw.
All inputs are finite; a program needn't handle non-finite values. No bound on the sum of `pro_live` on one device may be relied on, other than what follows from the above.
Results may differ from a plain program's by a relative error of at most 0.0003.
Values sent between devices are 32-bit elements; how exact they have to be, the bound alone decides.
A program may use at most 128 MiB of HBM per device.

v0:
```python
import jax
import jax.numpy as jnp
from jax import lax
from jax.sharding import PartitionSpec as P

COARSEN = 4


precise = lax.Precision.HIGHEST


def broadcast(value, axis, root):
    mine = lax.axis_index(axis) == root
    return lax.psum(jnp.where(mine, value, jnp.zeros_like(value)), axis)


def column_panel(masked_pro, pro_cols):
    return (
        lax.all_gather(masked_pro, "row", axis=0, tiled=True),
        lax.all_gather(pro_cols, "row", axis=0, tiled=True),
    )


def shards(op_tiles, op_rows, op_cols, op_count, pro_tiles, pro_cols, pro_live):
    list_len = op_tiles.shape[0]
    tile_size = op_tiles.shape[2]
    fine_rows = pro_tiles.shape[0]
    row_count = lax.axis_size("row")
    col_count = lax.axis_size("col")
    fine_total = fine_rows * row_count
    fine_cols = fine_total // col_count
    coarse_total = fine_total // COARSEN
    coarse_cols = coarse_total // col_count
    coarse_rows = coarse_total // row_count
    row_index = lax.axis_index("row")
    col_index = lax.axis_index("col")
    live_op = (jnp.arange(list_len, dtype=jnp.int32) < op_count[0, 0]).astype(jnp.float32)
    masked_op = op_tiles[:, 0] * live_op[:, None, None]
    masked_pro = pro_tiles * pro_live.astype(jnp.float32)[:, :, None, None]
    op_where = jnp.stack([op_rows[:, 0], op_cols[:, 0] + col_index * fine_cols], axis=1)
    panel_tiles, panel_ids = column_panel(masked_pro, pro_cols)
    empty_product = jnp.zeros((fine_rows, coarse_cols, tile_size, tile_size), jnp.float32)
    piece_tiles = lax.all_gather(masked_op, "col", axis=0, tiled=True)
    piece_where = lax.all_gather(op_where, "col", axis=0, tiled=True)
    fine_ids = piece_where[:, 1]
    right_tiles = panel_tiles[fine_ids, 0]
    targets = panel_ids[fine_ids, 0]
    tile_prods = jnp.einsum("nab,nbc->nac", piece_tiles, right_tiles, precision=precise)
    product = empty_product.at[piece_where[:, 0], targets].add(tile_prods)
    panel_tiles, panel_ids = column_panel(masked_pro, pro_cols)
    root_col = row_index * coarse_rows // coarse_cols
    far_tiles, far_ids = (
        broadcast(panel_tiles, "col", root_col),
        broadcast(panel_ids, "col", root_col),
    )
    shift_ids = root_col * coarse_cols - row_index * coarse_rows
    empty_owned = jnp.zeros((coarse_rows, coarse_cols, tile_size, tile_size), jnp.float32)
    left_tiles = far_tiles
    left_ids = far_ids + shift_ids
    inside = (left_ids >= 0) & (left_ids < coarse_rows)
    left_tiles = left_tiles * inside.astype(jnp.float32)[:, :, None, None]
    tile_prods = jnp.einsum(
        "ksba,kjbc->ksjac",
        left_tiles,
        lax.all_gather(product, "row", axis=0, tiled=True),
        precision=precise,
    )
    placed = jnp.clip(left_ids, 0, coarse_rows - 1)
    coarse = empty_owned.at[placed.reshape(-1)].add(
        tile_prods.reshape((-1,) + tile_prods.shape[2:])
    )
    return (product, coarse)


def solution(mesh):
    return jax.shard_map(
        shards,
        mesh=mesh,
        in_specs=(
            P("row", "col", None, None),
            P("row", "col"),
            P("row", "col"),
            P("row", "col"),
            P("row", "col", None, None),
            P("row", "col"),
            P("row", "col"),
        ),
        out_specs=(P("row", "col", None, None), P("row", "col", None, None)),
        check_vma=False,
    )
```

profile of v0, /device:TPU:1, one launch (start us, length us, event | category | flops | bytes accessed | tf_op | source)
XLA Modules:
  0.0 547.0 jit_solution(2243945836866424324)
XLA Ops:
  7.2 0.7 convert_bitcast_fusion
  7.9 1.7 broadcast_multiply_fusion
  10.3 2.3 bitcast_multiply_fusion
  12.8 0.7 broadcast_add_fusion
  13.4 0.7 add_bitcast_fusion
  14.1 30.4 %all-gather = s32[16,32,2]{1,2,0:T(2,128)S(1)} all-gather(s32[1,32,2]{1,2,0:T(2,128)S(1)} %add_bitcast_fusion), channel_id=1, replica_groups=mesh['row'=16,'col'=16] {'col'}, dimensions={0}, use_global_device_ids=true | all-gather | bytes 4352 | tf_op jit(solution)/shard_map/all_gather | solution.py:44
  44.6 1.3 dynamic-slice
  46.5 30.3 %all-gather.7.cloned.1.call-done = f32[128,1,64,64]{3,2,1,0:T(8,128)} async-done(((f32[8,1,64,64]{3,2,1,0:T(8,128)}), f32[128,1,64,64]{3,2,1,0:T(8,128)}) %all-gather.7.cloned.1.call-update) | async-done | bytes 2097168 | tf_op jit(solution)/shard_map/all_gather | solution.py:19
  76.8 2.8 broadcast_select_fusion
  79.7 0.1 bitcast_dynamic-update-slice_fusion
  79.8 8.3 %all-reduce.1 = s32[128]{0:T(128)S(1)} all-reduce(s32[128]{0:T(128)S(1)} %bitcast_dynamic-update-slice_fusion), channel_id=1, replica_groups=mesh['row'=16,'col'=16] {'row'}, use_global_device_ids=true, to_apply=%add.1 | all-reduce | flops 128 | bytes 1024
  88.1 3.5 gather_fusion
  91.7 11.7 %gather_fusion.1 = f32[512,64,64]{2,1,0:T(8,128)} fusion(f32[128,1,64,64]{3,2,1,0:T(8,128)} %all-gather.7.cloned.1.call-done, s32[512]{0:T(512)S(1)} %bitcast.41), kind=kCustom, calls=%fused_computation.1 | custom fusion | bytes 16781312 | tf_op jit(solution)/shard_map/gather | solution.py:46
  103.3 158.7 %all-gather.5.cloned.1.call-done = f32[512,64,64]{2,1,0:T(8,128)} async-done(((f32[32,64,64]{2,1,0:T(8,128)}), f32[512,64,64]{2,1,0:T(8,128)}) %all-gather.5.cloned.1.call-update) | async-done | bytes 8388624 | tf_op jit(solution)/shard_map/all_gather | solution.py:43
  262.1 23.9 %fusion.12 = f32[512,64,64]{2,1,0:T(8,128)} fusion(f32[512,64,64]{2,1,0:T(8,128)} %all-gather.5.cloned.1.call-done, f32[512,64,64]{2,1,0:T(8,128)} %gather_fusion.1), kind=kOutput, calls=%fused_computation.31 | convolution fusion | flops 1610612736 | bytes 25165824 | tf_op jit(solution)/shard_map/nab,nbc->nac/dot_general | solution.py:48
  286.0 55.8 %scatter_fusion = f32[8,2,64,64]{3,2,1,0:T(8,128)S(1)} fusion(f32[8,2,64,64]{3,2,1,0:T(8,128)S(1)} %broadcast_in_dim.6, s32[512]{0:T(512)S(1)} %bitcast.42, f32[512,64,64]{2,1,0:T(8,128)} %fusion.12), kind=kCustom, calls=%fused_computation.2 | custom fusion | flops 2097152 | bytes 25169920 | tf_op jit(solution)/shard_map/scatter-add | solution.py:49
  341.8 0.8 copy-done
  342.6 10.7 %psum.14 = s32[128,1]{0,1:T(1,128)S(1)} all-reduce(s32[128,1]{0,1:T(1,128)S(1)} %broadcast_select_fusion.1), channel_id=1, replica_groups=mesh['row'=16,'col'=16] {'col'}, use_global_device_ids=true, to_apply=%region_1.2 | all-reduce | flops 128 | bytes 1024 | tf_op jit(solution)/shard_map/psum | solution.py:14
  353.3 54.1 %all-reduce.4.cloned.1.call-done = f32[128,1,64,64]{3,2,1,0:T(8,128)} async-done(((f32[128,1,64,64]{3,2,1,0:T(8,128)}), f32[128,1,64,64]{3,2,1,0:T(8,128)}) %all-reduce.4.cloned.1.call-update) | async-done | bytes 2097168 | tf_op jit(solution)/shard_map/psum | solution.py:14
  407.4 87.7 %all-gather.9.cloned.1.call-done = f32[128,2,64,64]{3,2,1,0:T(8,128)} async-done(((f32[8,2,64,64]{3,2,1,0:T(8,128)}), f32[128,2,64,64]{3,2,1,0:T(8,128)}) %all-gather.9.cloned.1.call-update) | async-done | bytes 4194320 | tf_op jit(solution)/shard_map/all_gather | solution.py:65
  495.2 18.5 %fusion.3 = f32[128,2,64,64]{2,3,1,0:T(8,128)} fusion(f32[128,2,64,64]{3,2,1,0:T(8,128)} %all-gather.9.cloned.1.call-done, f32[128,1,64,64]{3,2,1,0:T(8,128)} %all-reduce.4.cloned.1.call-done, f32[128]{0:T(128)S(1)} %fusion.10), kind=kOutput, calls=%fused_computation.7 | convolution fusion | flops 805830656 | bytes 10486272 | tf_op jit(solution)/shard_map/ksba,kjbc->ksjac/dot_general | solution.py:62
  513.7 9.1 %copy.15 = f32[128,2,64,64]{3,2,1,0:T(8,128)} copy(f32[128,2,64,64]{2,3,1,0:T(8,128)} %fusion.3) | data formatting | bytes 8388608 | tf_op jit(solution)/shard_map/reshape | solution.py:70
  522.8 17.0 %scatter_fusion.1 = f32[2,2,64,64]{3,2,1,0:T(8,128)S(1)} fusion(f32[2,2,64,64]{3,2,1,0:T(8,128)S(1)} %broadcast_in_dim.7, s32[128]{0:T(128)S(1)} %fusion.11, f32[128,2,64,64]{3,2,1,0:T(8,128)} %copy.15), kind=kCustom, calls=%fused_computation.3 | custom fusion | flops 1048576 | bytes 12583424 | tf_op jit(solution)/shard_map/scatter-add | solution.py:69
  539.8 0.6 copy-done.1
  (23 shorter events, 0.4 us)
Async XLA Ops:
  7.2 72.5 %copy-start.2 = (s32[8,1]{0,1:T(1,128)S(1)}, s32[8,1]{0,1:T(1,128)}, u32[]{:S(2)}) copy-start(s32[8,1]{0,1:T(1,128)} %param.12) | copy-start | bytes 100
  7.2 69.6 %all-gather.7.cloned.1.call-start = ((), (), s32[]{:S(2)}) async-start(), calls=%async_computation.1 | async-start | bytes 4456448 | tf_op jit(solution)/shard_map/all_gather | solution.py:19
  9.6 252.4 %all-gather.5.cloned.1.call-start = ((), (), s32[]{:S(2)}) async-start(), calls=%async_computation | async-start | bytes 17825792 | tf_op jit(solution)/shard_map/all_gather | solution.py:43
  12.7 394.7 %all-reduce.4.cloned.1.call-start = ((), (), s32[]{:S(2)}) async-start(), calls=%async_computation.3 | async-start | bytes 8388608 | tf_op jit(solution)/shard_map/psum | solution.py:14
  79.6 415.5 %all-gather.9.cloned.1.call-start = ((), (), s32[]{:S(2)}) async-start(), calls=%async_computation.2 | async-start | bytes 8912896 | tf_op jit(solution)/shard_map/all_gather | solution.py:65
  341.8 0.8 copy-start
  539.8 0.7 copy-start.1
Sparse Core Ops, SparseCore 0:
  11.3 65.4 all-gather.6
  78.6 183.4 all-gather.4
  264.8 142.6 all-reduce.3
  410.6 84.5 all-gather.8
where the time goes:
time: 549 us; the launch traced here: 547 us
  waiting for transfers between devices  331 us (60%)
  other arithmetic  81.6 us (15%)
  blocking collectives  49.4 us (9%)
  matrix products  42.4 us (8%)
  local copies, waits for them, and re-layouts  27.2 us (5%)
  between operations  15.2 us (3%)
    all_gather x1, waiting for transfers between devices, shards(): piece_tiles = lax.all_gather(masked_op, 'col', axis=0, tiled=True)  159 us
    all_gather x1, waiting for transfers between devices, shards(): lax.all_gather(product, 'row', axis=0, tiled=True)  87.7 us
    scatter-add x1, other arithmetic, shards(): product = empty_product.at[piece_where[:, 0], targets].add(tile_prods)  55.8 us
    psum x1, waiting for transfers between devices, broadcast(): return lax.psum(jnp.where(mine, value, jnp.zeros_like(value)), axis)  54.1 us
    all_gather x1, blocking collectives, shards(): piece_where = lax.all_gather(op_where, 'col', axis=0, tiled=True)  30.4 us
    all_gather x1, waiting for transfers between devices, column_panel(): lax.all_gather(masked_pro, 'row', axis=0, tiled=True)  30.3 us
    dot_general x1, matrix products, shards(): jnp.einsum('nab,nbc->nac', piece_tiles, right_tiles, precision=precise)  23.9 us
    dot_general x1, matrix products, shards(): jnp.einsum('ksba,kjbc->ksjac', left_tiles, lax.all_gather(product, 'row',...  18.5 us
  transfers between devices with their start and end apart: 4, of which 4 were waited for; matrix products, arithmetic and copies ran while one was open for 19% of the time, Pallas kernels for 0%

commit v1 on v0

v1 whole, which is shorter than its diff:
```python
import functools

import jax
import jax.numpy as jnp
from jax import lax
from jax.experimental import pallas as pl
from jax.experimental.pallas import tpu as pltpu
from jax.sharding import PartitionSpec as P

MESH = pl.DeviceIdType.MESH
F32, BF16 = jnp.float32, jnp.bfloat16
UR = 264
UH = 136
LA = 32
HALF = ((0, 256), (256, 256))

A_ID, T_ID, Y_ID = 0, 1, 2
X_ID = 3
CORE_ID = 11
Z_ID = 19
PY_ID = 27
RS_ID = 35
CC_ID = 51
CX_ID = 53
CY_ID = 57
N_ID = 58


def split(v):
    hi = v.astype(BF16)
    return hi, (v - hi.astype(F32)).astype(BF16)


def pack(tile):
    return jnp.concatenate([tile[:32], tile[32:]], axis=1)


def kernel(
    op_ref, rows_ref, cols_ref, count_ref, pro_ref, pcols_ref, plive_ref,
    prod_ref, coarse_ref,
    unit, alist, anear, panel, pror, ahi, alo, rhi, rlo, q, rsr, rsl, pthi, ptlo, phi, plo,
    cpart, crecv, xr0, xl0, xr1, xl1, yrecv,
    ssem, rsem, lsem,
):
    r = lax.axis_index("row")
    c = lax.axis_index("col")
    yh, x, core = r // 8, lax.rem(r // 2, 4), lax.rem(r, 2)
    yl, z = c // 8, lax.rem(c, 8)

    def rowdev(yh_, x_, core_):
        return ((yh_ * 4 + x_) * 2 + core_, c)

    ynear = (r, (1 - yl) * 8 + z)
    zright, zleft = (r, yl * 8 + lax.rem(z + 1, 8)), (r, yl * 8 + lax.rem(z + 7, 8))
    xright, xleft = rowdev(yh, lax.rem(x + 1, 4), core), rowdev(yh, lax.rem(x + 3, 4), core)
    yfar = rowdev(1 - yh, x, core)
    other = rowdev(yh, x, 1 - core)
    s0 = 2 * x + core
    across = ((yh * 4 + z // 2) * 2 + lax.rem(z, 2), yl * 8 + s0)
    own_across = s0 == z

    def send(src, dst, k, dev):
        pltpu.make_async_remote_copy(
            src_ref=src, dst_ref=dst, send_sem=ssem.at[k], recv_sem=rsem.at[k], device_id=dev, device_id_type=MESH
        ).start()

    def arrived(dst, k):
        pltpu.make_async_remote_copy(
            src_ref=dst, dst_ref=dst, send_sem=ssem.at[k], recv_sem=rsem.at[k], device_id=ynear, device_id_type=MESH
        ).wait_recv()

    def sent(src, k):
        pltpu.make_async_remote_copy(
            src_ref=src, dst_ref=src, send_sem=ssem.at[k], recv_sem=rsem.at[k], device_id=ynear, device_id_type=MESH
        ).wait_send()

    barrier = pltpu.get_barrier_semaphore()
    for dev in (ynear, zright, zleft, xright, xleft, yfar, other):
        pl.semaphore_signal(barrier, inc=1, device_id=dev, device_id_type=MESH)

    @pl.when(jnp.logical_not(own_across))
    def _():
        pl.semaphore_signal(barrier, inc=1, device_id=across, device_id_type=MESH)

    for k in range(8):
        live = plive_ref[k, 0].astype(F32)
        unit[pl.ds(k * 32, 32), :] = pack(pro_ref[k]) * live
        unit[pl.ds(256 + k, 1), :] = jnp.full((1, 128), pcols_ref[k, 0].astype(F32))

    pl.semaphore_wait(barrier, jnp.where(own_across, 7, 8))

    @pl.when(own_across)
    def _():
        pltpu.make_async_copy(unit, panel.at[yh, z], lsem.at[0]).start()

    @pl.when(jnp.logical_not(own_across))
    def _():
        send(unit, panel.at[yh, z], T_ID, across)

    keep = pltpu.make_async_copy(unit, pror.at[yl, z], lsem.at[1])
    keep.start()

    def pack_slot(t, carry):
        alist[t] = pack(op_ref[t])
        pos = jnp.where(t < count_ref[0, 0], rows_ref[t, 0] * 8 + cols_ref[t, 0], -1)
        alist[LA, pl.ds(t, 1), :] = jnp.full((1, 128), pos.astype(F32))
        return carry

    lax.fori_loop(0, LA, pack_slot, 0)
    send(alist, anear, A_ID, ynear)

    left32 = lax.broadcasted_iota(jnp.int32, (32, 128), 1) < 64

    def build_a(src, at):
        def row(i, carry):
            base = (i * 8).astype(F32)

            def slot(t, accs):
                tile = src[t]
                pos = src[LA, pl.ds(t, 1), :]
                return tuple(
                    acc + jnp.where(jnp.broadcast_to(pos == base + float(k), (32, 128)), tile, 0.0)
                    for k, acc in enumerate(accs)
                )

            accs = lax.fori_loop(0, LA, slot, tuple(jnp.zeros((32, 128), F32) for _ in range(8)))
            for m in range(4):
                even, odd = accs[2 * m], accs[2 * m + 1]
                top = jnp.where(left32, even, pltpu.roll(odd, 64, 1))
                bot = jnp.where(left32, pltpu.roll(even, 64, 1), odd)
                for off, v in ((0, top), (32, bot)):
                    hi, lo = split(v)
                    at_rows = pl.ds(pl.multiple_of(i * 64 + off, 32), 32)
                    ahi[at, at_rows, pl.ds(m * 128, 128)] = hi
                    alo[at, at_rows, pl.ds(m * 128, 128)] = lo
            return carry

        lax.fori_loop(0, 8, row, 0)

    build_a(alist, yl)

    def dense(ref, b, s, k):
        tile = ref[b, s, pl.ds(k * 32, 32), :]
        col = ref[b, s, pl.ds(256 + k, 1), :]
        turned = pltpu.roll(tile, 64, 1)
        a, bb = 1.0 - col, col
        top = jnp.where(left32, tile * a, turned * bb)
        bot = jnp.where(left32, turned * a, tile * bb)
        return top, bot

    @pl.when(own_across)
    def _():
        pltpu.make_async_copy(unit, panel.at[yh, z], lsem.at[0]).wait()

    @pl.when(jnp.logical_not(own_across))
    def _():
        arrived(panel.at[yh, s0], T_ID)

    sl, sr = lax.rem(s0 + 6, 8), lax.rem(s0 + 2, 8)
    sf = lax.rem(s0 + 4, 8)
    lo_half, hi_half = pl.ds(0, UH), pl.ds(UH, UR - UH)

    def spread(b, k):
        u = panel.at[b, s0]
        send(u, u, k, xright)
        send(u, u, k + 1, xleft)

    mine, theirs = yh, 1 - yh
    u = panel.at[mine, s0]
    send(u, u, Y_ID, yfar)
    spread(mine, X_ID)
    send(u, u, CORE_ID, other)
    keep.wait()
    zu = pror.at[yl, z]
    send(zu, zu, Z_ID, zright)
    send(zu, zu, Z_ID + 4, zleft)
    send(zu, zu, PY_ID, ynear)

    def pass_on(b, k, kc):
        u = panel.at[b, sl]
        arrived(u, k)
        send(u.at[lo_half], u.at[lo_half], k + 2, xright)
        send(u, u, kc, other)
        u = panel.at[b, sr]
        arrived(u, k + 1)
        send(u.at[hi_half], u.at[hi_half], k + 3, xleft)
        send(u, u, kc + 1, other)

    def zstep(step):
        got_r = pror.at[yl, lax.rem(z + 8 - step, 8)]
        got_l = pror.at[yl, lax.rem(z + step, 8)]
        arrived(got_r, Z_ID + step - 1)
        arrived(got_l, Z_ID + 4 + step - 1)
        if step < 3:
            send(got_r, got_r, Z_ID + step, zright)
            send(got_l, got_l, Z_ID + 4 + step, zleft)
        else:
            send(got_r.at[lo_half], got_r.at[lo_half], Z_ID + 3, zright)
            send(got_l.at[hi_half], got_l.at[hi_half], Z_ID + 7, zleft)
        send(got_r, got_r, PY_ID + 2 * step - 1, ynear)
        send(got_l, got_l, PY_ID + 2 * step, ynear)

    pass_on(mine, X_ID, CORE_ID + 1)
    u = panel.at[theirs, s0]
    arrived(u, Y_ID)
    spread(theirs, X_ID + 4)
    send(u, u, CORE_ID + 4, other)
    zstep(1)
    far = panel.at[mine, sf]
    arrived(far.at[lo_half], X_ID + 2)
    arrived(far.at[hi_half], X_ID + 3)
    send(far, far, CORE_ID + 3, other)
    pass_on(theirs, X_ID + 4, CORE_ID + 5)
    zstep(2)
    arrived(anear, A_ID)
    build_a(anear, 1 - yl)
    far2 = panel.at[theirs, sf]
    arrived(far2.at[lo_half], X_ID + 6)
    arrived(far2.at[hi_half], X_ID + 7)
    send(far2, far2, CORE_ID + 7, other)
    zstep(3)
    o0 = 2 * x + 1 - core
    from_other = [
        panel.at[b, lax.rem(o0 + off, 8)] for b in (mine, theirs) for off in (0, 6, 2, 4)
    ]
    for n, ref in enumerate(from_other):
        arrived(ref, CORE_ID + n)

    def build_r(d, at):
        s = lax.rem(z + d, 8)

        def block(b, carry):
            for k in range(8):
                for off, v in zip((0, 32), dense(panel, b, s, k)):
                    hi, lo = split(v)
                    rhi[b, pl.ds(k * 64 + off, 32), pl.ds(at * 128, 128)] = hi
                    rlo[b, pl.ds(k * 64 + off, 32), pl.ds(at * 128, 128)] = lo
            return carry

        lax.fori_loop(0, 2, block, 0)

    def dot(a, b):
        return lax.dot_general(a, b, (((1,), (0,)), ((), ())), preferred_element_type=F32)

    def chunk(d0, d1):
        build_r(d0, 0)
        build_r(d1, 1)

        def part(m, carry):
            rows = pl.ds(pl.multiple_of(m * 256, 256), 256)
            acc = jnp.zeros((256, 256), F32)
            for b in range(2):
                h, l = ahi[b, rows, :], alo[b, rows, :]
                acc = acc + dot(h, rhi[b]) + dot(h, rlo[b]) + dot(l, rhi[b])
            q[d0, rows, :] = acc[:, :128]
            q[d1, rows, :] = acc[:, 128:]
            return carry

        lax.fori_loop(0, 2, part, 0)

    def rs_id(step, half, way):
        return RS_ID + (step * 2 + half) * 2 + way

    def rs_send(d, step, half, way):
        rows = pl.ds(*HALF[half])
        buf = (rsr, rsl)[way]
        send(q.at[d, rows], buf.at[step, rows], rs_id(step, half, way), (zright, zleft)[way])

    def rs_add(d, step, half, way):
        rows = pl.ds(*HALF[half])
        buf = (rsr, rsl)[way]
        arrived(buf.at[step, rows], rs_id(step, half, way))
        q[d, rows, :] = q[d, rows, :] + buf[step, rows, :]

    def build_t(b, s):
        for m in range(4):
            t0, b0 = dense(pror, b, s, 2 * m)
            t1, b1 = dense(pror, b, s, 2 * m + 1)
            v = jnp.concatenate([t0, b0, t1, b1], axis=0).T
            hi, lo = split(v)
            pthi[b * 8 + s, :, pl.ds(m * 128, 128)] = hi
            ptlo[b * 8 + s, :, pl.ds(m * 128, 128)] = lo

    chunk(4, 0)
    rs_send(4, 0, 0, 0)
    rs_send(4, 0, 1, 1)
    chunk(3, 5)
    rs_send(3, 1, 1, 0)
    rs_send(5, 1, 0, 1)
    rs_add(3, 0, 0, 0)
    rs_send(3, 1, 0, 0)
    rs_add(5, 0, 1, 1)
    rs_send(5, 1, 1, 1)
    chunk(2, 6)

    zfar = pror.at[yl, lax.rem(z + 4, 8)]
    arrived(zfar.at[lo_half], Z_ID + 3)
    arrived(zfar.at[hi_half], Z_ID + 7)
    send(zfar, zfar, PY_ID + 7, ynear)

    for half_r, half_l in ((1, 0), (0, 1)):
        rs_add(2, 1, half_r, 0)
        rs_send(2, 2, half_r, 0)
        rs_add(6, 1, half_l, 1)
        rs_send(6, 2, half_l, 1)
    chunk(1, 7)

    def own_t(s, carry):
        build_t(yl, s)
        return carry

    for half_r, half_l in ((1, 0), (0, 1)):
        rs_add(1, 2, half_r, 0)
        rs_send(1, 3, half_r, 0)
        rs_add(7, 2, half_l, 1)
        rs_send(7, 3, half_l, 1)
    lax.fori_loop(0, 8, own_t, 0)

    near = [pror.at[1 - yl, z]]
    for step in (1, 2, 3):
        near += [pror.at[1 - yl, lax.rem(z + 8 - step, 8)], pror.at[1 - yl, lax.rem(z + step, 8)]]
    near.append(pror.at[1 - yl, lax.rem(z + 4, 8)])
    for n, ref in enumerate(near):
        arrived(ref, PY_ID + n)

    def near_t(s, carry):
        build_t(1 - yl, s)
        return carry

    lax.fori_loop(0, 8, near_t, 0)

    for half in (0, 1):
        rs_add(0, 3, half, 0)
        rs_add(0, 3, half, 1)
        rows = pl.ds(*HALF[half])
        hi, lo = split(q[0, rows, :])
        phi[rows, :] = hi
        plo[rows, :] = lo

    def coarse_part(gc):
        def one(g, carry):
            at = g * 2 + gc
            h, l = pthi[at], ptlo[at]
            v = dot(h, phi[...]) + dot(h, plo[...]) + dot(l, phi[...])
            cpart[gc, lax.rem(g, 4), g // 4] = v
            return carry

        lax.fori_loop(0, 8, one, 0)

    coarse_part(1 - core)
    send(cpart.at[1 - core], crecv, CC_ID, other)
    coarse_part(core)
    for i in range(8):
        v = q[0, pl.ds(i * 64, 64), :]
        prod_ref[i, 0] = v[:, :64]
        prod_ref[i, 1] = v[:, 64:]
    arrived(crecv, CC_ID)

    def add_core(n, carry):
        cpart[core, n] = cpart[core, n] + crecv[n]
        return carry

    x2 = lax.rem(x + 2, 4)
    xp, xm = lax.rem(x + 1, 4), lax.rem(x + 3, 4)
    cp = cpart.at[core]
    add_core(x2, 0)
    send(cp.at[x2, 0], xr0, CX_ID, xright)
    send(cp.at[x2, 1], xl0, CX_ID + 1, xleft)
    add_core(xp, 0)
    add_core(xm, 0)
    add_core(x, 0)
    arrived(xr0, CX_ID)
    cpart[core, xp, 0] = cpart[core, xp, 0] + xr0[...]
    send(cp.at[xp], xr1, CX_ID + 2, xright)
    arrived(xl0, CX_ID + 1)
    cpart[core, xm, 1] = cpart[core, xm, 1] + xl0[...]
    send(cp.at[xm], xl1, CX_ID + 3, xleft)
    arrived(xr1, CX_ID + 2)
    arrived(xl1, CX_ID + 3)
    cpart[core, x, 1 - yh] = cpart[core, x, 1 - yh] + xr1[1 - yh] + xl1[1 - yh]
    send(cp.at[x, 1 - yh], yrecv, CY_ID, yfar)
    total = cpart[core, x, yh] + xr1[yh] + xl1[yh]
    arrived(yrecv, CY_ID)
    total = total + yrecv[...]
    for a in range(2):
        for b in range(2):
            coarse_ref[a, b] = total[a * 64 : a * 64 + 64, b * 64 : b * 64 + 64]

    @pl.when(jnp.logical_not(own_across))
    def _():
        sent(unit, T_ID)

    sent(alist, A_ID)
    u = panel.at[0, 0]
    zu = pror.at[0, 0]
    sent(u, Y_ID)
    for k in (X_ID, X_ID + 4):
        sent(u, k)
        sent(u, k + 1)
        sent(u.at[lo_half], k + 2)
        sent(u.at[hi_half], k + 3)
    for n in range(8):
        sent(u, CORE_ID + n)
        sent(zu, PY_ID + n)
    for n in range(3):
        sent(zu, Z_ID + n)
        sent(zu, Z_ID + 4 + n)
    sent(zu.at[lo_half], Z_ID + 3)
    sent(zu.at[hi_half], Z_ID + 7)
    piece = q.at[0, pl.ds(0, 256)]
    sent(piece, rs_id(0, 0, 0))
    sent(piece, rs_id(0, 1, 1))
    for step in (1, 2, 3):
        for half in (0, 1):
            for way in (0, 1):
                sent(piece, rs_id(step, half, way))
    sent(crecv, CC_ID)
    sent(xr0, CX_ID)
    sent(xl0, CX_ID + 1)
    sent(xr1, CX_ID + 2)
    sent(xl1, CX_ID + 3)
    sent(yrecv, CY_ID)


def shards(op_tiles, op_rows, op_cols, op_count, pro_tiles, pro_cols, pro_live):
    vmem = pl.BlockSpec(memory_space=pltpu.VMEM)
    smem = pl.BlockSpec(memory_space=pltpu.SMEM)
    return pl.pallas_call(
        kernel,
        out_shape=(
            jax.ShapeDtypeStruct((8, 2, 64, 64), F32),
            jax.ShapeDtypeStruct((2, 2, 64, 64), F32),
        ),
        in_specs=[vmem, smem, smem, smem, vmem, smem, smem],
        out_specs=(vmem, vmem),
        scratch_shapes=[
            pltpu.VMEM((UR, 128), F32),
            pltpu.VMEM((LA + 1, 32, 128), F32),
            pltpu.VMEM((LA + 1, 32, 128), F32),
            pltpu.VMEM((2, 8, UR, 128), F32),
            pltpu.VMEM((2, 8, UR, 128), F32),
            pltpu.VMEM((2, 512, 512), BF16),
            pltpu.VMEM((2, 512, 512), BF16),
            pltpu.VMEM((2, 512, 256), BF16),
            pltpu.VMEM((2, 512, 256), BF16),
            pltpu.VMEM((8, 512, 128), F32),
            pltpu.VMEM((4, 512, 128), F32),
            pltpu.VMEM((4, 512, 128), F32),
            pltpu.VMEM((16, 128, 512), BF16),
            pltpu.VMEM((16, 128, 512), BF16),
            pltpu.VMEM((512, 128), BF16),
            pltpu.VMEM((512, 128), BF16),
            pltpu.VMEM((2, 4, 2, 128, 128), F32),
            pltpu.VMEM((4, 2, 128, 128), F32),
            pltpu.VMEM((128, 128), F32),
            pltpu.VMEM((128, 128), F32),
            pltpu.VMEM((2, 128, 128), F32),
            pltpu.VMEM((2, 128, 128), F32),
            pltpu.VMEM((128, 128), F32),
            pltpu.SemaphoreType.DMA((N_ID,)),
            pltpu.SemaphoreType.DMA((N_ID,)),
            pltpu.SemaphoreType.DMA((2,)),
        ],
        compiler_params=pltpu.CompilerParams(
            collective_id=0, has_side_effects=True, vmem_limit_bytes=60 * 1024 * 1024
        ),
    )(
        op_tiles.reshape(32, 64, 64), op_rows, op_cols, op_count,
        pro_tiles.reshape(8, 64, 64), pro_cols, pro_live,
    )


def solution(mesh):
    return jax.shard_map(
        shards,
        mesh=mesh,
        in_specs=(
            P("row", "col", None, None),
            P("row", "col"),
            P("row", "col"),
            P("row", "col"),
            P("row", "col", None, None),
            P("row", "col"),
            P("row", "col"),
        ),
        out_specs=(P("row", "col", None, None), P("row", "col", None, None)),
        check_vma=False,
    )
```

time: 549 us -> 92.3 us (0.17)
  waiting for transfers between devices: 331 us -> 0 us
  Pallas kernels: 0 us -> 84.7 us
  other arithmetic: 81.6 us -> 0 us
  blocking collectives: 49.4 us -> 0 us
  matrix products: 42.4 us -> 0 us
  local copies, waits for them, and re-layouts: 27.2 us -> 5.94 us
  between operations: 15.2 us -> 1.31 us
    all_gather x3 -> x0, waiting for transfers between devices: 277 us -> none  [the longest x1 159 us: shards(): piece_tiles = lax.all_gather(masked_op, 'col', axis=0, tiled=True)]
    pallas_call x0 -> x1, Pallas kernels: none -> 84.7 us  [shards(): pl.pallas_call(kernel, out_shape=(jax.ShapeDtypeStruct((8, 2, 64, 64), F3...]
    scatter-add x2 -> x0, other arithmetic: 72.8 us -> none  [the longest x1 55.8 us: shards(): product = empty_product.at[piece_where[:, 0], targets].add(tile_prods)]
    psum x1 -> x0, waiting for transfers between devices: 54.1 us -> none  [broadcast(): return lax.psum(jnp.where(mine, value, jnp.zeros_like(value)), axis)]
    dot_general x2 -> x0, matrix products: 42.4 us -> none  [the longest x1 23.9 us: shards(): jnp.einsum('nab,nbc->nac', piece_tiles, right_tiles, precision=precise)]
    all_gather x1 -> x0, blocking collectives: 30.4 us -> none  [shards(): piece_where = lax.all_gather(op_where, 'col', axis=0, tiled=True)]
    gather x2 -> x0, local copies, waits for them, and re-layouts: 15.2 us -> none  [the longest x1 11.7 us: shards(): right_tiles = panel_tiles[fine_ids, 0]]
    psum x1 -> x0, blocking collectives: 10.7 us -> none  [broadcast(): return lax.psum(jnp.where(mine, value, jnp.zeros_like(value)), axis)]
  transfers between devices with their start and end apart: 4 -> 0, of which waited for: 4 -> 0; matrix products, arithmetic and copies ran while one was open for 19% -> 0% of each run, Pallas kernels for 0% -> 0%
where the time goes in v1:
time: 92.3 us; the launch traced here: 91.9 us
  Pallas kernels  84.7 us (92%)
  local copies, waits for them, and re-layouts  5.94 us (6%)
  between operations  1.31 us (1%)
    pallas_call x1, Pallas kernels, shards(): pl.pallas_call(kernel, out_shape=(jax.ShapeDtypeStruct((8, 2, 64, 64), F3...  84.7 us
    unnamed x16, local copies, waits for them, and re-layouts  5.94 us

profile of v1, /device:TPU:1, one launch (start us, length us, event | category | flops | bytes accessed | tf_op | source)
XLA Modules:
  0.0 91.9 jit_solution(15163896429478360123)
XLA Ops:
  1.3 0.0 copy-start.1
  1.3 0.6 copy-done.1
  1.9 0.0 copy-start.2
  1.9 0.7 copy.11.pcols_ref
  2.6 0.0 copy-done.2
  2.6 0.0 copy-start.3
  2.6 0.7 copy.12.plive_ref
  3.3 0.0 copy-done.3
  3.3 0.0 copy-start.4
  3.3 0.7 copy.9.rows_ref
  4.0 0.0 copy-done.4
  4.0 0.7 copy.10.cols_ref
  4.7 84.7 %shard_map.86 = (f32[8,2,64,64]{3,2,1,0:T(8,128)}, f32[2,2,64,64]{3,2,1,0:T(8,128)}) custom-call(f32[32,64,64]{2,1,0:T(8,128)} %bitcast.2, s32[32,1]{1,0:T(8,128)} %copy.9.rows_ref, s32[32,1]{1,0:T(8,128)} %copy.10.cols_ref, s32[1,1]{1,0:T(1,128)S(6)} %copy.15.count_ref, f32[8,64,64]{2,1,0:T(8,128)} %bitcast.3, s32[8,1]{1,0:T(8,128)} %copy.11.pcols_ref, ...), custom_call_target="tpu_custom_call" | custom-call | tf_op jit(solution)/shard_map/pallas_call | solution.py:428
  89.3 0.0 copy-start
  89.3 1.9 %copy.16 = f32[8,2,64,64]{3,2,1,0:T(8,128)} copy(f32[8,2,64,64]{3,2,1,0:T(8,128)} %get-tuple-element.4) | data formatting | bytes 524288
  91.3 0.0 copy-done
  91.3 0.7 copy.17
Async XLA Ops:
  1.3 0.7 copy-start.1
  1.9 0.7 copy-start.2
  2.6 0.7 copy-start.3
  3.3 0.7 copy-start.4
  89.3 1.9 %copy-start = (f32[2,2,64,64]{3,2,1,0:T(8,128)S(1)}, f32[2,2,64,64]{3,2,1,0:T(8,128)}, u32[]{:S(2)}) copy-start(f32[2,2,64,64]{3,2,1,0:T(8,128)} %get-tuple-element.5) | copy-start | bytes 196612

commit v2 on v1

--- a/solution.py
+++ b/solution.py
@@ -14,16 +14,17 @@
 LA = 32
 HALF = ((0, 256), (256, 256))
 
-A_ID, T_ID, Y_ID = 0, 1, 2
+M_ID, T_ID, Y_ID = 0, 1, 2
 X_ID = 3
 CORE_ID = 11
 Z_ID = 19
 PY_ID = 27
 RS_ID = 35
 CC_ID = 51
-CX_ID = 53
-CY_ID = 57
-N_ID = 58
+CX_ID = 55
+CY_ID = 59
+A_ID = 60
+N_ID = 64
 
 
 def split(v):
@@ -36,9 +37,10 @@
 
 
 def kernel(
-    op_ref, rows_ref, cols_ref, count_ref, pro_ref, pcols_ref, plive_ref,
-    prod_ref, coarse_ref,
-    unit, alist, anear, panel, pror, ahi, alo, rhi, rlo, q, rsr, rsl, pthi, ptlo, phi, plo,
+    op_hbm, rows_ref, cols_ref, count_ref, pro_ref, pcols_ref, plive_ref,
+    prod_hbm, coarse_ref,
+    op_ref, prod_ref, meta, mnear,
+    unit, alist, anear, panel, pror, ahi, alo, rhi, rlo, q, rsr, rsl, pthi, ptlo, pcat,
     cpart, crecv, xr0, xl0, xr1, xl1, yrecv,
     ssem, rsem, lsem,
 ):
@@ -74,6 +76,8 @@
             src_ref=src, dst_ref=src, send_sem=ssem.at[k], recv_sem=rsem.at[k], device_id=ynear, device_id_type=MESH
         ).wait_send()
 
+    fetch = pltpu.make_async_copy(op_hbm, op_ref, lsem.at[2])
+    fetch.start()
     barrier = pltpu.get_barrier_semaphore()
     for dev in (ynear, zright, zleft, xright, xleft, yfar, other):
         pl.semaphore_signal(barrier, inc=1, device_id=dev, device_id_type=MESH)
@@ -83,9 +87,9 @@
         pl.semaphore_signal(barrier, inc=1, device_id=across, device_id_type=MESH)
 
     for k in range(8):
-        live = plive_ref[k, 0].astype(F32)
+        live = plive_ref[0, k].astype(F32)
         unit[pl.ds(k * 32, 32), :] = pack(pro_ref[k]) * live
-        unit[pl.ds(256 + k, 1), :] = jnp.full((1, 128), pcols_ref[k, 0].astype(F32))
+        unit[pl.ds(256 + k, 1), :] = jnp.full((1, 128), pcols_ref[0, k].astype(F32))
 
     pl.semaphore_wait(barrier, jnp.where(own_across, 7, 8))
 
@@ -100,44 +104,65 @@
     keep = pltpu.make_async_copy(unit, pror.at[yl, z], lsem.at[1])
     keep.start()
 
-    def pack_slot(t, carry):
-        alist[t] = pack(op_ref[t])
-        pos = jnp.where(t < count_ref[0, 0], rows_ref[t, 0] * 8 + cols_ref[t, 0], -1)
-        alist[LA, pl.ds(t, 1), :] = jnp.full((1, 128), pos.astype(F32))
-        return carry
-
-    lax.fori_loop(0, LA, pack_slot, 0)
-    send(alist, anear, A_ID, ynear)
+    pos = rows_ref[...] * 8 + cols_ref[...]
+    live_slot = lax.broadcasted_iota(jnp.int32, (1, LA), 1) < count_ref[0, 0]
+    pos = jnp.where(live_slot, pos, -1).astype(F32)
+    meta[...] = jnp.zeros((8, 128), F32)
+    meta[pl.ds(0, 1), pl.ds(0, LA)] = pos
+    meta[pl.ds(0, 1), pl.ds(LA, LA)] = pos
+    send(meta, mnear, M_ID, ynear)
+    fetch.wait()
+
+    def pack_piece(n):
+        def slot(t, carry):
+            a = op_ref[t, pl.ds(n * 8, 8), :]
+            b = op_ref[t, pl.ds(32 + n * 8, 8), :]
+            alist[pl.ds(n * 8, 8), t, :] = jnp.concatenate([a, b], axis=1)
+            return carry
+
+        lax.fori_loop(0, LA, slot, 0, unroll=8)
+
+    def send_piece(n):
+        at = pl.ds(n * 8, 8)
+        send(alist.at[at], anear.at[at], A_ID + n, ynear)
+
+    for n in range(4):
+        pack_piece(n)
+        if n < 2:
+            send_piece(n)
 
     left32 = lax.broadcasted_iota(jnp.int32, (32, 128), 1) < 64
-
-    def build_a(src, at):
-        def row(i, carry):
-            base = (i * 8).astype(F32)
-
-            def slot(t, accs):
-                tile = src[t]
-                pos = src[LA, pl.ds(t, 1), :]
-                return tuple(
-                    acc + jnp.where(jnp.broadcast_to(pos == base + float(k), (32, 128)), tile, 0.0)
-                    for k, acc in enumerate(accs)
-                )
-
-            accs = lax.fori_loop(0, LA, slot, tuple(jnp.zeros((32, 128), F32) for _ in range(8)))
-            for m in range(4):
-                even, odd = accs[2 * m], accs[2 * m + 1]
-                top = jnp.where(left32, even, pltpu.roll(odd, 64, 1))
-                bot = jnp.where(left32, pltpu.roll(even, 64, 1), odd)
-                for off, v in ((0, top), (32, bot)):
-                    hi, lo = split(v)
-                    at_rows = pl.ds(pl.multiple_of(i * 64 + off, 32), 32)
+    left8 = lax.broadcasted_iota(jnp.int32, (8, 128), 1) < 64
+    place = lax.broadcasted_iota(jnp.int32, (64, 2 * LA), 0)
+    place = (lax.rem(place, 8) * 8 + place // 8).astype(F32)
+
+    def dot(a, b):
+        return lax.dot_general(a, b, (((1,), (0,)), ((), ())), preferred_element_type=F32)
+
+    def build_a(src, which, at, n):
+        hot = (which[pl.ds(0, 1), pl.ds(0, 2 * LA)] == place).astype(F32).astype(BF16)
+
+        def row(step, carry):
+            rho = n * 8 + step * 2
+            h0, l0 = split(src[rho])
+            h1, l1 = split(src[rho + 1])
+            both = jnp.concatenate(
+                [jnp.concatenate([h0, l0], axis=0), jnp.concatenate([h1, l1], axis=0)], axis=1
+            )
+            tiles = dot(hot, both)
+            for e in range(2):
+                t = tiles[:, e * 128 : e * 128 + 128]
+                for m in range(4):
+                    even, odd = t[m * 16 : m * 16 + 8], t[m * 16 + 8 : m * 16 + 16]
+                    top = jnp.where(left8, even, pltpu.roll(odd, 64, 1))
+                    bot = jnp.where(left8, pltpu.roll(even, 64, 1), odd)
+                    hi, lo = split(jnp.concatenate([top, bot], axis=0))
+                    at_rows = pl.ds(pl.multiple_of((rho + e) * 16, 16), 16)
                     ahi[at, at_rows, pl.ds(m * 128, 128)] = hi
                     alo[at, at_rows, pl.ds(m * 128, 128)] = lo
             return carry
 
-        lax.fori_loop(0, 8, row, 0)
-
-    build_a(alist, yl)
+        lax.fori_loop(0, 4, row, 0)
 
     def dense(ref, b, s, k):
         tile = ref[b, s, pl.ds(k * 32, 32), :]
@@ -148,6 +173,8 @@
         bot = jnp.where(left32, turned * a, tile * bb)
         return top, bot
 
+    build_a(alist, meta, yl, 0)
+
     @pl.when(own_across)
     def _():
         pltpu.make_async_copy(unit, panel.at[yh, z], lsem.at[0]).wait()
@@ -168,13 +195,14 @@
     mine, theirs = yh, 1 - yh
     u = panel.at[mine, s0]
     send(u, u, Y_ID, yfar)
+    send_piece(2)
+    send_piece(3)
     spread(mine, X_ID)
     send(u, u, CORE_ID, other)
     keep.wait()
     zu = pror.at[yl, z]
     send(zu, zu, Z_ID, zright)
     send(zu, zu, Z_ID + 4, zleft)
-    send(zu, zu, PY_ID, ynear)
 
     def pass_on(b, k, kc):
         u = panel.at[b, sl]
@@ -197,28 +225,39 @@
         else:
             send(got_r.at[lo_half], got_r.at[lo_half], Z_ID + 3, zright)
             send(got_l.at[hi_half], got_l.at[hi_half], Z_ID + 7, zleft)
-        send(got_r, got_r, PY_ID + 2 * step - 1, ynear)
-        send(got_l, got_l, PY_ID + 2 * step, ynear)
-
+
+    for n in range(1, 4):
+        build_a(alist, meta, yl, n)
     pass_on(mine, X_ID, CORE_ID + 1)
     u = panel.at[theirs, s0]
     arrived(u, Y_ID)
     spread(theirs, X_ID + 4)
     send(u, u, CORE_ID + 4, other)
     zstep(1)
+    arrived(mnear, M_ID)
+    for n in range(2):
+        arrived(anear.at[pl.ds(n * 8, 8)], A_ID + n)
+        build_a(anear, mnear, 1 - yl, n)
     far = panel.at[mine, sf]
     arrived(far.at[lo_half], X_ID + 2)
     arrived(far.at[hi_half], X_ID + 3)
     send(far, far, CORE_ID + 3, other)
     pass_on(theirs, X_ID + 4, CORE_ID + 5)
     zstep(2)
-    arrived(anear, A_ID)
-    build_a(anear, 1 - yl)
     far2 = panel.at[theirs, sf]
     arrived(far2.at[lo_half], X_ID + 6)
     arrived(far2.at[hi_half], X_ID + 7)
     send(far2, far2, CORE_ID + 7, other)
     zstep(3)
+    for n in range(2, 4):
+        arrived(anear.at[pl.ds(n * 8, 8)], A_ID + n)
+        build_a(anear, mnear, 1 - yl, n)
+    send(zu, zu, PY_ID, ynear)
+    for step in (1, 2, 3):
+        got_r = pror.at[yl, lax.rem(z + 8 - step, 8)]
+        got_l = pror.at[yl, lax.rem(z + step, 8)]
+        send(got_r, got_r, PY_ID + 2 * step - 1, ynear)
+        send(got_l, got_l, PY_ID + 2 * step, ynear)
     o0 = 2 * x + 1 - core
     from_other = [
         panel.at[b, lax.rem(o0 + off, 8)] for b in (mine, theirs) for off in (0, 6, 2, 4)
@@ -238,9 +277,6 @@
             return carry
 
         lax.fori_loop(0, 2, block, 0)
-
-    def dot(a, b):
-        return lax.dot_general(a, b, (((1,), (0,)), ((), ())), preferred_element_type=F32)
 
     def chunk(d0, d1):
         build_r(d0, 0)
@@ -273,13 +309,19 @@
         q[d, rows, :] = q[d, rows, :] + buf[step, rows, :]
 
     def build_t(b, s):
+        flag = pror[b, s, pl.ds(256, 8), :]
         for m in range(4):
-            t0, b0 = dense(pror, b, s, 2 * m)
-            t1, b1 = dense(pror, b, s, 2 * m + 1)
-            v = jnp.concatenate([t0, b0, t1, b1], axis=0).T
-            hi, lo = split(v)
-            pthi[b * 8 + s, :, pl.ds(m * 128, 128)] = hi
-            ptlo[b * 8 + s, :, pl.ds(m * 128, 128)] = lo
+            parts = []
+            for rho in range(8 * m, 8 * m + 8):
+                tile = pror[b, s, pl.ds(rho, 8, stride=32), :]
+                turned = pltpu.roll(tile, 64, 1)
+                parts.append(jnp.where(left8, tile * (1.0 - flag), turned * flag))
+                parts.append(jnp.where(left8, turned * (1.0 - flag), tile * flag))
+            hi, lo = split(jnp.concatenate(parts, axis=0).T)
+            g = b * 8 + s
+            rows = pl.ds(pl.multiple_of(g // 8 * 128, 128), 128)
+            pthi[lax.rem(g, 2), lax.rem(g // 2, 4), rows, pl.ds(m * 128, 128)] = hi
+            ptlo[lax.rem(g, 2), lax.rem(g // 2, 4), rows, pl.ds(m * 128, 128)] = lo
 
     chunk(4, 0)
     rs_send(4, 0, 0, 0)
@@ -334,47 +376,50 @@
         rs_add(0, 3, half, 1)
         rows = pl.ds(*HALF[half])
         hi, lo = split(q[0, rows, :])
-        phi[rows, :] = hi
-        plo[rows, :] = lo
-
-    def coarse_part(gc):
-        def one(g, carry):
-            at = g * 2 + gc
-            h, l = pthi[at], ptlo[at]
-            v = dot(h, phi[...]) + dot(h, plo[...]) + dot(l, phi[...])
-            cpart[gc, lax.rem(g, 4), g // 4] = v
-            return carry
-
-        lax.fori_loop(0, 8, one, 0)
-
-    coarse_part(1 - core)
-    send(cpart.at[1 - core], crecv, CC_ID, other)
-    coarse_part(core)
-    for i in range(8):
-        v = q[0, pl.ds(i * 64, 64), :]
-        prod_ref[i, 0] = v[:, :64]
-        prod_ref[i, 1] = v[:, 64:]
-    arrived(crecv, CC_ID)
-
-    def add_core(n, carry):
-        cpart[core, n] = cpart[core, n] + crecv[n]
-        return carry
+        pcat[rows, pl.ds(0, 128)] = hi
+        pcat[rows, pl.ds(128, 128)] = lo
+
+    def coarse_part(gc, gx):
+        v = dot(pthi[gc, gx], pcat[...])
+        v = v[:, :128] + v[:, 128:] + dot(ptlo[gc, gx], pcat[:, :128])
+        cpart[gc, gx, 0] = v[:128]
+        cpart[gc, gx, 1] = v[128:]
+
+    def to_other(gx, n):
+        coarse_part(1 - core, gx)
+        send(cpart.at[1 - core, gx], crecv.at[gx], CC_ID + n, other)
+
+    def from_core(gx, n):
+        coarse_part(core, gx)
+        arrived(crecv.at[gx], CC_ID + n)
+        cpart[core, gx] = cpart[core, gx] + crecv[gx]
 
     x2 = lax.rem(x + 2, 4)
     xp, xm = lax.rem(x + 1, 4), lax.rem(x + 3, 4)
     cp = cpart.at[core]
-    add_core(x2, 0)
+    to_other(x2, 0)
+    to_other(xp, 1)
+    from_core(x2, 0)
     send(cp.at[x2, 0], xr0, CX_ID, xright)
     send(cp.at[x2, 1], xl0, CX_ID + 1, xleft)
-    add_core(xp, 0)
-    add_core(xm, 0)
-    add_core(x, 0)
+    to_other(xm, 2)
+    from_core(xp, 1)
+    to_other(x, 3)
+    from_core(xm, 2)
     arrived(xr0, CX_ID)
     cpart[core, xp, 0] = cpart[core, xp, 0] + xr0[...]
     send(cp.at[xp], xr1, CX_ID + 2, xright)
     arrived(xl0, CX_ID + 1)
     cpart[core, xm, 1] = cpart[core, xm, 1] + xl0[...]
     send(cp.at[xm], xl1, CX_ID + 3, xleft)
+    from_core(x, 3)
+    for i in range(8):
+        for h in range(2):
+            v = q[0, pl.ds(h * 8 + i, 32, stride=16), :]
+            prod_ref[i, 0, pl.ds(h * 32, 32), :] = v[:, :64]
+            prod_ref[i, 1, pl.ds(h * 32, 32), :] = v[:, 64:]
+    put = pltpu.make_async_copy(prod_ref, prod_hbm, lsem.at[3])
+    put.start()
     arrived(xr1, CX_ID + 2)
     arrived(xl1, CX_ID + 3)
     cpart[core, x, 1 - yh] = cpart[core, x, 1 - yh] + xr1[1 - yh] + xl1[1 - yh]
@@ -390,7 +435,10 @@
     def _():
         sent(unit, T_ID)
 
-    sent(alist, A_ID)
+    put.wait()
+    sent(meta, M_ID)
+    for n in range(4):
+        sent(alist.at[pl.ds(0, 8)], A_ID + n)
     u = panel.at[0, 0]
     zu = pror.at[0, 0]
     sent(u, Y_ID)
@@ -414,7 +462,8 @@
         for half in (0, 1):
             for way in (0, 1):
                 sent(piece, rs_id(step, half, way))
-    sent(crecv, CC_ID)
+    for n in range(4):
+        sent(crecv.at[0], CC_ID + n)
     sent(xr0, CX_ID)
     sent(xl0, CX_ID + 1)
     sent(xr1, CX_ID + 2)
@@ -425,18 +474,23 @@
 def shards(op_tiles, op_rows, op_cols, op_count, pro_tiles, pro_cols, pro_live):
     vmem = pl.BlockSpec(memory_space=pltpu.VMEM)
     smem = pl.BlockSpec(memory_space=pltpu.SMEM)
+    anywhere = pl.BlockSpec(memory_space=pl.ANY)
     return pl.pallas_call(
         kernel,
         out_shape=(
             jax.ShapeDtypeStruct((8, 2, 64, 64), F32),
             jax.ShapeDtypeStruct((2, 2, 64, 64), F32),
         ),
-        in_specs=[vmem, smem, smem, smem, vmem, smem, smem],
-        out_specs=(vmem, vmem),
+        in_specs=[anywhere, vmem, vmem, smem, vmem, smem, smem],
+        out_specs=(anywhere, vmem),
         scratch_shapes=[
+            pltpu.VMEM((LA, 64, 64), F32),
+            pltpu.VMEM((8, 2, 64, 64), F32),
+            pltpu.VMEM((8, 128), F32),
+            pltpu.VMEM((8, 128), F32),
             pltpu.VMEM((UR, 128), F32),
-            pltpu.VMEM((LA + 1, 32, 128), F32),
-            pltpu.VMEM((LA + 1, 32, 128), F32),
+            pltpu.VMEM((32, LA, 128), F32),
+            pltpu.VMEM((32, LA, 128), F32),
             pltpu.VMEM((2, 8, UR, 128), F32),
             pltpu.VMEM((2, 8, UR, 128), F32),
             pltpu.VMEM((2, 512, 512), BF16),
@@ -446,10 +500,9 @@
             pltpu.VMEM((8, 512, 128), F32),
             pltpu.VMEM((4, 512, 128), F32),
             pltpu.VMEM((4, 512, 128), F32),
-            pltpu.VMEM((16, 128, 512), BF16),
-            pltpu.VMEM((16, 128, 512), BF16),
-            pltpu.VMEM((512, 128), BF16),
-            pltpu.VMEM((512, 128), BF16),
+            pltpu.VMEM((2, 4, 256, 512), BF16),
+            pltpu.VMEM((2, 4, 256, 512), BF16),
+            pltpu.VMEM((512, 256), BF16),
             pltpu.VMEM((2, 4, 2, 128, 128), F32),
             pltpu.VMEM((4, 2, 128, 128), F32),
             pltpu.VMEM((128, 128), F32),
@@ -459,14 +512,14 @@
             pltpu.VMEM((128, 128), F32),
             pltpu.SemaphoreType.DMA((N_ID,)),
             pltpu.SemaphoreType.DMA((N_ID,)),
-            pltpu.SemaphoreType.DMA((2,)),
+            pltpu.SemaphoreType.DMA((4,)),
         ],
         compiler_params=pltpu.CompilerParams(
             collective_id=0, has_side_effects=True, vmem_limit_bytes=60 * 1024 * 1024
         ),
     )(
-        op_tiles.reshape(32, 64, 64), op_rows, op_cols, op_count,
-        pro_tiles.reshape(8, 64, 64), pro_cols, pro_live,
+        op_tiles.reshape(32, 64, 64), op_rows.T, op_cols.T, op_count,
+        pro_tiles.reshape(8, 64, 64), pro_cols.T, pro_live.T,
     )
 
 

time: 92.3 us -> 84 us (0.910)
  Pallas kernels: 84.7 us -> 80 us
  local copies, waits for them, and re-layouts: 5.94 us -> 2.58 us
    pallas_call x1, Pallas kernels: 84.7 us -> 80 us  [shards(): pl.pallas_call(kernel, out_shape=(jax.ShapeDtypeStruct((8, 2, 64, 64), F3...]
    unnamed x16 -> x4, local copies, waits for them, and re-layouts: 5.94 us -> 2.58 us
where the time goes in v2:
time: 84 us; the launch traced here: 83.9 us
  Pallas kernels  80 us (95%)
  local copies, waits for them, and re-layouts  2.58 us (3%)
  between operations  1.29 us (2%)
    pallas_call x1, Pallas kernels, shards(): pl.pallas_call(kernel, out_shape=(jax.ShapeDtypeStruct((8, 2, 64, 64), F3...  80 us
    unnamed x4, local copies, waits for them, and re-layouts  2.58 us

profile of v2, /device:TPU:1, one launch (start us, length us, event | category | flops | bytes accessed | tf_op | source)
XLA Modules:
  0.0 83.9 jit_solution(10365859869865439678)
XLA Ops:
  1.3 80.0 %shard_map.86 = (f32[8,2,64,64]{3,2,1,0:T(8,128)}, f32[2,2,64,64]{3,2,1,0:T(8,128)}) custom-call(f32[32,64,64]{2,1,0:T(8,128)} %bitcast.6, s32[1,32]{1,0:T(1,128)} %bitcast.8, s32[1,32]{1,0:T(1,128)} %bitcast.9, s32[1,1]{1,0:T(1,128)S(6)} %copy.11.count_ref, f32[8,64,64]{2,1,0:T(8,128)} %bitcast.7, s32[1,8]{1,0:T(1,128)} %bitcast.10, s32[1,8]{1,0:T(1,128)} %bitcast.11), custom_call_target="tpu_custom_call" | custom-call | tf_op jit(solution)/shard_map/pallas_call | solution.py:478
  81.3 0.0 copy-start
  81.3 1.9 %copy.12 = f32[8,2,64,64]{3,2,1,0:T(8,128)} copy(f32[8,2,64,64]{3,2,1,0:T(8,128)} %get-tuple-element.4) | data formatting | bytes 524288
  83.2 0.0 copy-done
  83.2 0.7 copy.13
Async XLA Ops:
  81.3 1.9 %copy-start = (f32[2,2,64,64]{3,2,1,0:T(8,128)S(1)}, f32[2,2,64,64]{3,2,1,0:T(8,128)}, u32[]{:S(2)}) copy-start(f32[2,2,64,64]{3,2,1,0:T(8,128)} %get-tuple-element.5) | copy-start | bytes 196612

commit v3 on v2

--- a/solution.py
+++ b/solution.py
@@ -13,18 +13,21 @@
 UH = 136
 LA = 32
 HALF = ((0, 256), (256, 256))
-
-M_ID, T_ID, Y_ID = 0, 1, 2
-X_ID = 3
-CORE_ID = 11
-Z_ID = 19
-PY_ID = 27
-RS_ID = 35
-CC_ID = 51
-CX_ID = 55
-CY_ID = 59
-A_ID = 60
-N_ID = 64
+PART = (pl.ds(0, UH), pl.ds(UH, UR - UH))
+
+M_ID = 0
+A_ID = 1
+T_ID = 5
+Y_ID = 7
+X_ID = 9
+CORE_ID = 21
+Z_ID = 29
+PY_ID = 37
+RS_ID = 45
+CC_ID = 61
+CX_ID = 65
+CY_ID = 73
+N_ID = 75
 
 
 def split(v):
@@ -57,9 +60,11 @@
     xright, xleft = rowdev(yh, lax.rem(x + 1, 4), core), rowdev(yh, lax.rem(x + 3, 4), core)
     yfar = rowdev(1 - yh, x, core)
     other = rowdev(yh, x, 1 - core)
-    s0 = 2 * x + core
-    across = ((yh * 4 + z // 2) * 2 + lax.rem(z, 2), yl * 8 + s0)
-    own_across = s0 == z
+    s0 = 4 * core + x
+    plane = 2 * x + core
+    across = rowdev(yh, lax.rem(z, 4), z // 4)[0], yl * 8 + plane
+    source = rowdev(yh, z // 2, lax.rem(z, 2))[0], yl * 8 + s0
+    own_across = jnp.logical_and(s0 == z, plane == z)
 
     def send(src, dst, k, dev):
         pltpu.make_async_remote_copy(
@@ -85,13 +90,14 @@
     @pl.when(jnp.logical_not(own_across))
     def _():
         pl.semaphore_signal(barrier, inc=1, device_id=across, device_id_type=MESH)
+        pl.semaphore_signal(barrier, inc=1, device_id=source, device_id_type=MESH)
 
     for k in range(8):
         live = plive_ref[0, k].astype(F32)
         unit[pl.ds(k * 32, 32), :] = pack(pro_ref[k]) * live
         unit[pl.ds(256 + k, 1), :] = jnp.full((1, 128), pcols_ref[0, k].astype(F32))
 
-    pl.semaphore_wait(barrier, jnp.where(own_across, 7, 8))
+    pl.semaphore_wait(barrier, jnp.where(own_across, 7, 9))
 
     @pl.when(own_across)
     def _():
@@ -99,7 +105,8 @@
 
     @pl.when(jnp.logical_not(own_across))
     def _():
-        send(unit, panel.at[yh, z], T_ID, across)
+        for p in range(2):
+            send(unit.at[PART[p]], panel.at[yh, z].at[PART[p]], T_ID + p, across)
 
     keep = pltpu.make_async_copy(unit, pror.at[yl, z], lsem.at[1])
     keep.start()
@@ -175,44 +182,38 @@
 
     build_a(alist, meta, yl, 0)
 
-    @pl.when(own_across)
-    def _():
-        pltpu.make_async_copy(unit, panel.at[yh, z], lsem.at[0]).wait()
-
-    @pl.when(jnp.logical_not(own_across))
-    def _():
-        arrived(panel.at[yh, s0], T_ID)
-
-    sl, sr = lax.rem(s0 + 6, 8), lax.rem(s0 + 2, 8)
-    sf = lax.rem(s0 + 4, 8)
-    lo_half, hi_half = pl.ds(0, UH), pl.ds(UH, UR - UH)
-
-    def spread(b, k):
-        u = panel.at[b, s0]
-        send(u, u, k, xright)
-        send(u, u, k + 1, xleft)
+    def ring(off):
+        return 4 * core + lax.rem(x + off, 4)
 
     mine, theirs = yh, 1 - yh
-    u = panel.at[mine, s0]
-    send(u, u, Y_ID, yfar)
-    send_piece(2)
-    send_piece(3)
-    spread(mine, X_ID)
-    send(u, u, CORE_ID, other)
-    keep.wait()
-    zu = pror.at[yl, z]
-    send(zu, zu, Z_ID, zright)
-    send(zu, zu, Z_ID + 4, zleft)
-
-    def pass_on(b, k, kc):
+    sl, sr, sf = ring(3), ring(1), ring(2)
+
+    def spread(b, k, p):
+        u = panel.at[b, s0].at[PART[p]]
+        send(u, u, k + p, xright)
+        send(u, u, k + 2 + p, xleft)
+
+    def onward(b, k):
+        u = panel.at[b, sl].at[PART[0]]
+        arrived(u, k)
+        send(u, u, k + 4, xright)
+        u = panel.at[b, sr].at[PART[1]]
+        arrived(u, k + 3)
+        send(u, u, k + 5, xleft)
+
+    def beside(b, k, kc):
         u = panel.at[b, sl]
-        arrived(u, k)
-        send(u.at[lo_half], u.at[lo_half], k + 2, xright)
-        send(u, u, kc, other)
+        arrived(u.at[PART[1]], k + 1)
+        send(u, u, kc + 1, other)
         u = panel.at[b, sr]
-        arrived(u, k + 1)
-        send(u.at[hi_half], u.at[hi_half], k + 3, xleft)
-        send(u, u, kc + 1, other)
+        arrived(u.at[PART[0]], k + 2)
+        send(u, u, kc + 2, other)
+
+    def far(b, k, kc):
+        u = panel.at[b, sf]
+        arrived(u.at[PART[0]], k + 4)
+        arrived(u.at[PART[1]], k + 5)
+        send(u, u, kc + 3, other)
 
     def zstep(step):
         got_r = pror.at[yl, lax.rem(z + 8 - step, 8)]
@@ -223,47 +224,58 @@
             send(got_r, got_r, Z_ID + step, zright)
             send(got_l, got_l, Z_ID + 4 + step, zleft)
         else:
-            send(got_r.at[lo_half], got_r.at[lo_half], Z_ID + 3, zright)
-            send(got_l.at[hi_half], got_l.at[hi_half], Z_ID + 7, zleft)
-
-    for n in range(1, 4):
-        build_a(alist, meta, yl, n)
-    pass_on(mine, X_ID, CORE_ID + 1)
+            send(got_r.at[PART[0]], got_r.at[PART[0]], Z_ID + 3, zright)
+            send(got_l.at[PART[1]], got_l.at[PART[1]], Z_ID + 7, zleft)
+        send(got_r, got_r, PY_ID + 2 * step - 1, ynear)
+        send(got_l, got_l, PY_ID + 2 * step, ynear)
+
+    u = panel.at[mine, s0]
+
+    @pl.when(own_across)
+    def _():
+        pltpu.make_async_copy(unit, panel.at[yh, z], lsem.at[0]).wait()
+
+    for p in range(2):
+        @pl.when(jnp.logical_not(own_across))
+        def _():
+            arrived(u.at[PART[p]], T_ID + p)
+
+        send(u.at[PART[p]], u.at[PART[p]], Y_ID + p, yfar)
+        spread(mine, X_ID, p)
+    send_piece(2)
+    send_piece(3)
+    send(u, u, CORE_ID, other)
+    keep.wait()
+    zu = pror.at[yl, z]
+    send(zu, zu, Z_ID, zright)
+    send(zu, zu, Z_ID + 4, zleft)
+    send(zu, zu, PY_ID, ynear)
+    build_a(alist, meta, yl, 1)
+    onward(mine, X_ID)
+    build_a(alist, meta, yl, 2)
     u = panel.at[theirs, s0]
-    arrived(u, Y_ID)
-    spread(theirs, X_ID + 4)
+    for p in range(2):
+        arrived(u.at[PART[p]], Y_ID + p)
+        spread(theirs, X_ID + 6, p)
     send(u, u, CORE_ID + 4, other)
+    beside(mine, X_ID, CORE_ID)
     zstep(1)
+    build_a(alist, meta, yl, 3)
+    onward(theirs, X_ID + 6)
+    far(mine, X_ID, CORE_ID)
     arrived(mnear, M_ID)
     for n in range(2):
         arrived(anear.at[pl.ds(n * 8, 8)], A_ID + n)
         build_a(anear, mnear, 1 - yl, n)
-    far = panel.at[mine, sf]
-    arrived(far.at[lo_half], X_ID + 2)
-    arrived(far.at[hi_half], X_ID + 3)
-    send(far, far, CORE_ID + 3, other)
-    pass_on(theirs, X_ID + 4, CORE_ID + 5)
+    beside(theirs, X_ID + 6, CORE_ID + 4)
     zstep(2)
-    far2 = panel.at[theirs, sf]
-    arrived(far2.at[lo_half], X_ID + 6)
-    arrived(far2.at[hi_half], X_ID + 7)
-    send(far2, far2, CORE_ID + 7, other)
-    zstep(3)
+    far(theirs, X_ID + 6, CORE_ID + 4)
     for n in range(2, 4):
         arrived(anear.at[pl.ds(n * 8, 8)], A_ID + n)
         build_a(anear, mnear, 1 - yl, n)
-    send(zu, zu, PY_ID, ynear)
-    for step in (1, 2, 3):
-        got_r = pror.at[yl, lax.rem(z + 8 - step, 8)]
-        got_l = pror.at[yl, lax.rem(z + step, 8)]
-        send(got_r, got_r, PY_ID + 2 * step - 1, ynear)
-        send(got_l, got_l, PY_ID + 2 * step, ynear)
-    o0 = 2 * x + 1 - core
-    from_other = [
-        panel.at[b, lax.rem(o0 + off, 8)] for b in (mine, theirs) for off in (0, 6, 2, 4)
-    ]
-    for n, ref in enumerate(from_other):
-        arrived(ref, CORE_ID + n)
+    for n in range(8):
+        s = 4 * (1 - core) + lax.rem(x + (0, 3, 1, 2)[n % 4], 4)
+        arrived(panel.at[(mine, theirs)[n // 4], s], CORE_ID + n)
 
     def build_r(d, at):
         s = lax.rem(z + d, 8)
@@ -326,6 +338,7 @@
     chunk(4, 0)
     rs_send(4, 0, 0, 0)
     rs_send(4, 0, 1, 1)
+    zstep(3)
     chunk(3, 5)
     rs_send(3, 1, 1, 0)
     rs_send(5, 1, 0, 1)
@@ -336,8 +349,8 @@
     chunk(2, 6)
 
     zfar = pror.at[yl, lax.rem(z + 4, 8)]
-    arrived(zfar.at[lo_half], Z_ID + 3)
-    arrived(zfar.at[hi_half], Z_ID + 7)
+    arrived(zfar.at[PART[0]], Z_ID + 3)
+    arrived(zfar.at[PART[1]], Z_ID + 7)
     send(zfar, zfar, PY_ID + 7, ynear)
 
     for half_r, half_l in ((1, 0), (0, 1)):
@@ -400,18 +413,21 @@
     to_other(x2, 0)
     to_other(xp, 1)
     from_core(x2, 0)
-    send(cp.at[x2, 0], xr0, CX_ID, xright)
-    send(cp.at[x2, 1], xl0, CX_ID + 1, xleft)
+    top_bot = (pl.ds(0, 64), pl.ds(64, 64))
+    for h, rows in enumerate(top_bot):
+        send(cp.at[x2, 0, rows], xr0.at[rows], CX_ID + h, xright)
+        send(cp.at[x2, 1, rows], xl0.at[rows], CX_ID + 2 + h, xleft)
     to_other(xm, 2)
     from_core(xp, 1)
     to_other(x, 3)
     from_core(xm, 2)
-    arrived(xr0, CX_ID)
-    cpart[core, xp, 0] = cpart[core, xp, 0] + xr0[...]
-    send(cp.at[xp], xr1, CX_ID + 2, xright)
-    arrived(xl0, CX_ID + 1)
-    cpart[core, xm, 1] = cpart[core, xm, 1] + xl0[...]
-    send(cp.at[xm], xl1, CX_ID + 3, xleft)
+    for h, rows in enumerate(top_bot):
+        arrived(xr0.at[rows], CX_ID + h)
+        cpart[core, xp, 0, rows] = cpart[core, xp, 0, rows] + xr0[rows]
+        send(cp.at[xp, :, rows], xr1.at[:, rows], CX_ID + 4 + h, xright)
+        arrived(xl0.at[rows], CX_ID + 2 + h)
+        cpart[core, xm, 1, rows] = cpart[core, xm, 1, rows] + xl0[rows]
+        send(cp.at[xm, :, rows], xl1.at[:, rows], CX_ID + 6 + h, xleft)
     from_core(x, 3)
     for i in range(8):
         for h in range(2):
@@ -420,41 +436,44 @@
             prod_ref[i, 1, pl.ds(h * 32, 32), :] = v[:, 64:]
     put = pltpu.make_async_copy(prod_ref, prod_hbm, lsem.at[3])
     put.start()
-    arrived(xr1, CX_ID + 2)
-    arrived(xl1, CX_ID + 3)
-    cpart[core, x, 1 - yh] = cpart[core, x, 1 - yh] + xr1[1 - yh] + xl1[1 - yh]
-    send(cp.at[x, 1 - yh], yrecv, CY_ID, yfar)
-    total = cpart[core, x, yh] + xr1[yh] + xl1[yh]
-    arrived(yrecv, CY_ID)
-    total = total + yrecv[...]
-    for a in range(2):
+    for h, rows in enumerate(top_bot):
+        arrived(xr1.at[:, rows], CX_ID + 4 + h)
+        arrived(xl1.at[:, rows], CX_ID + 6 + h)
+        cpart[core, x, 1 - yh, rows] = cpart[core, x, 1 - yh, rows] + xr1[1 - yh, rows] + xl1[1 - yh, rows]
+        send(cp.at[x, 1 - yh, rows], yrecv.at[rows], CY_ID + h, yfar)
+    for h, rows in enumerate(top_bot):
+        total = cpart[core, x, yh, rows] + xr1[yh, rows] + xl1[yh, rows]
+        arrived(yrecv.at[rows], CY_ID + h)
+        total = total + yrecv[rows]
         for b in range(2):
-            coarse_ref[a, b] = total[a * 64 : a * 64 + 64, b * 64 : b * 64 + 64]
-
-    @pl.when(jnp.logical_not(own_across))
-    def _():
-        sent(unit, T_ID)
-
+            coarse_ref[h, b] = total[:, b * 64 : b * 64 + 64]
+
+    u = panel.at[0, 0]
+    zu = pror.at[0, 0]
+    for p in range(2):
+        part = u.at[PART[p]]
+
+        @pl.when(jnp.logical_not(own_across))
+        def _():
+            sent(part, T_ID + p)
+
+        sent(part, Y_ID + p)
+        for k in (X_ID, X_ID + 6):
+            sent(part, k + p)
+            sent(part, k + 2 + p)
+            sent(part, k + 4 + p)
     put.wait()
     sent(meta, M_ID)
     for n in range(4):
         sent(alist.at[pl.ds(0, 8)], A_ID + n)
-    u = panel.at[0, 0]
-    zu = pror.at[0, 0]
-    sent(u, Y_ID)
-    for k in (X_ID, X_ID + 4):
-        sent(u, k)
-        sent(u, k + 1)
-        sent(u.at[lo_half], k + 2)
-        sent(u.at[hi_half], k + 3)
     for n in range(8):
         sent(u, CORE_ID + n)
         sent(zu, PY_ID + n)
     for n in range(3):
         sent(zu, Z_ID + n)
         sent(zu, Z_ID + 4 + n)
-    sent(zu.at[lo_half], Z_ID + 3)
-    sent(zu.at[hi_half], Z_ID + 7)
+    sent(zu.at[PART[0]], Z_ID + 3)
+    sent(zu.at[PART[1]], Z_ID + 7)
     piece = q.at[0, pl.ds(0, 256)]
     sent(piece, rs_id(0, 0, 0))
     sent(piece, rs_id(0, 1, 1))
@@ -464,11 +483,12 @@
                 sent(piece, rs_id(step, half, way))
     for n in range(4):
         sent(crecv.at[0], CC_ID + n)
-    sent(xr0, CX_ID)
-    sent(xl0, CX_ID + 1)
-    sent(xr1, CX_ID + 2)
-    sent(xl1, CX_ID + 3)
-    sent(yrecv, CY_ID)
+    for h, rows in enumerate(top_bot):
+        sent(xr0.at[rows], CX_ID + h)
+        sent(xl0.at[rows], CX_ID + 2 + h)
+        sent(xr1.at[:, rows], CX_ID + 4 + h)
+        sent(xl1.at[:, rows], CX_ID + 6 + h)
+        sent(yrecv.at[rows], CY_ID + h)
 
 
 def shards(op_tiles, op_rows, op_cols, op_count, pro_tiles, pro_cols, pro_live):

time: 84 us -> 82.1 us (0.977)
  Pallas kernels: 80 us -> 78.1 us
    pallas_call x1, Pallas kernels: 80 us -> 78.1 us  [shards(): pl.pallas_call(kernel, out_shape=(jax.ShapeDtypeStruct((8, 2, 64, 64), F3...]
where the time goes in v3:
time: 82.1 us; the launch traced here: 81.9 us
  Pallas kernels  78.1 us (95%)
  local copies, waits for them, and re-layouts  2.58 us (3%)
  between operations  1.29 us (2%)
    pallas_call x1, Pallas kernels, shards(): pl.pallas_call(kernel, out_shape=(jax.ShapeDtypeStruct((8, 2, 64, 64), F3...  78.1 us
    unnamed x4, local copies, waits for them, and re-layouts  2.58 us

profile of v3, /device:TPU:1, one launch (start us, length us, event | category | flops | bytes accessed | tf_op | source)
XLA Modules:
  0.0 81.9 jit_solution(2507574003713606346)
XLA Ops:
  1.3 78.1 %shard_map.86 = (f32[8,2,64,64]{3,2,1,0:T(8,128)}, f32[2,2,64,64]{3,2,1,0:T(8,128)}) custom-call(f32[32,64,64]{2,1,0:T(8,128)} %bitcast.6, s32[1,32]{1,0:T(1,128)} %bitcast.8, s32[1,32]{1,0:T(1,128)} %bitcast.9, s32[1,1]{1,0:T(1,128)S(6)} %copy.11.count_ref, f32[8,64,64]{2,1,0:T(8,128)} %bitcast.7, s32[1,8]{1,0:T(1,128)} %bitcast.10, s32[1,8]{1,0:T(1,128)} %bitcast.11), custom_call_target="tpu_custom_call" | custom-call | tf_op jit(solution)/shard_map/pallas_call | solution.py:498
  79.3 0.0 copy-start
  79.3 1.9 %copy.12 = f32[8,2,64,64]{3,2,1,0:T(8,128)} copy(f32[8,2,64,64]{3,2,1,0:T(8,128)} %get-tuple-element.4) | data formatting | bytes 524288
  81.3 0.0 copy-done
  81.3 0.7 copy.13
Async XLA Ops:
  79.3 1.9 %copy-start = (f32[2,2,64,64]{3,2,1,0:T(8,128)S(1)}, f32[2,2,64,64]{3,2,1,0:T(8,128)}, u32[]{:S(2)}) copy-start(f32[2,2,64,64]{3,2,1,0:T(8,128)} %get-tuple-element.5) | copy-start | bytes 196612

commit v4 on v3

--- a/solution.py
+++ b/solution.py
@@ -60,9 +60,10 @@
     xright, xleft = rowdev(yh, lax.rem(x + 1, 4), core), rowdev(yh, lax.rem(x + 3, 4), core)
     yfar = rowdev(1 - yh, x, core)
     other = rowdev(yh, x, 1 - core)
-    s0 = 4 * core + x
+    turn = 8 - z // 2 - 2 * lax.rem(z, 2)
+    s0 = 4 * core + lax.rem(x + turn, 4)
     plane = 2 * x + core
-    across = rowdev(yh, lax.rem(z, 4), z // 4)[0], yl * 8 + plane
+    across = rowdev(yh, lax.rem(z + x + 2 * core, 4), z // 4)[0], yl * 8 + plane
     source = rowdev(yh, z // 2, lax.rem(z, 2))[0], yl * 8 + s0
     own_across = jnp.logical_and(s0 == z, plane == z)
 
@@ -180,10 +181,13 @@
         bot = jnp.where(left32, turned * a, tile * bb)
         return top, bot
 
+    zu = pror.at[yl, z]
+    send(unit, zu, Z_ID, zright)
+    send(unit, zu, Z_ID + 4, zleft)
     build_a(alist, meta, yl, 0)
 
     def ring(off):
-        return 4 * core + lax.rem(x + off, 4)
+        return 4 * core + lax.rem(x + turn + off, 4)
 
     mine, theirs = yh, 1 - yh
     sl, sr, sf = ring(3), ring(1), ring(2)
@@ -246,10 +250,8 @@
     send_piece(3)
     send(u, u, CORE_ID, other)
     keep.wait()
-    zu = pror.at[yl, z]
-    send(zu, zu, Z_ID, zright)
-    send(zu, zu, Z_ID + 4, zleft)
     send(zu, zu, PY_ID, ynear)
+    zstep(1)
     build_a(alist, meta, yl, 1)
     onward(mine, X_ID)
     build_a(alist, meta, yl, 2)
@@ -259,8 +261,8 @@
         spread(theirs, X_ID + 6, p)
     send(u, u, CORE_ID + 4, other)
     beside(mine, X_ID, CORE_ID)
-    zstep(1)
     build_a(alist, meta, yl, 3)
+    zstep(2)
     onward(theirs, X_ID + 6)
     far(mine, X_ID, CORE_ID)
     arrived(mnear, M_ID)
@@ -268,13 +270,13 @@
         arrived(anear.at[pl.ds(n * 8, 8)], A_ID + n)
         build_a(anear, mnear, 1 - yl, n)
     beside(theirs, X_ID + 6, CORE_ID + 4)
-    zstep(2)
+    zstep(3)
     far(theirs, X_ID + 6, CORE_ID + 4)
     for n in range(2, 4):
         arrived(anear.at[pl.ds(n * 8, 8)], A_ID + n)
         build_a(anear, mnear, 1 - yl, n)
     for n in range(8):
-        s = 4 * (1 - core) + lax.rem(x + (0, 3, 1, 2)[n % 4], 4)
+        s = 4 * (1 - core) + lax.rem(x + turn + (0, 3, 1, 2)[n % 4], 4)
         arrived(panel.at[(mine, theirs)[n // 4], s], CORE_ID + n)
 
     def build_r(d, at):
@@ -289,6 +291,21 @@
             return carry
 
         lax.fori_loop(0, 2, block, 0)
+
+    def chunk_one(d):
+        build_r(d, 0)
+
+        def part(m, carry):
+            rows = pl.ds(pl.multiple_of(m * 256, 256), 256)
+            acc = jnp.zeros((256, 128), F32)
+            for b in range(2):
+                h, l = ahi[b, rows, :], alo[b, rows, :]
+                rh = rhi[b, :, pl.ds(0, 128)]
+                acc = acc + dot(h, rh) + dot(h, rlo[b, :, pl.ds(0, 128)]) + dot(l, rh)
+            q[d, rows, :] = acc
+            return carry
+
+        lax.fori_loop(0, 2, part, 0)
 
     def chunk(d0, d1):
         build_r(d0, 0)
@@ -335,10 +352,9 @@
             pthi[lax.rem(g, 2), lax.rem(g // 2, 4), rows, pl.ds(m * 128, 128)] = hi
             ptlo[lax.rem(g, 2), lax.rem(g // 2, 4), rows, pl.ds(m * 128, 128)] = lo
 
-    chunk(4, 0)
+    chunk_one(4)
     rs_send(4, 0, 0, 0)
     rs_send(4, 0, 1, 1)
-    zstep(3)
     chunk(3, 5)
     rs_send(3, 1, 1, 0)
     rs_send(5, 1, 0, 1)
@@ -346,12 +362,12 @@
     rs_send(3, 1, 0, 0)
     rs_add(5, 0, 1, 1)
     rs_send(5, 1, 1, 1)
-    chunk(2, 6)
-
     zfar = pror.at[yl, lax.rem(z + 4, 8)]
     arrived(zfar.at[PART[0]], Z_ID + 3)
     arrived(zfar.at[PART[1]], Z_ID + 7)
     send(zfar, zfar, PY_ID + 7, ynear)
+
+    chunk(2, 6)
 
     for half_r, half_l in ((1, 0), (0, 1)):
         rs_add(2, 1, half_r, 0)
@@ -369,6 +385,7 @@
         rs_send(1, 3, half_r, 0)
         rs_add(7, 2, half_l, 1)
         rs_send(7, 3, half_l, 1)
+    chunk_one(0)
     lax.fori_loop(0, 8, own_t, 0)
 
     near = [pror.at[1 - yl, z]]

time: 82.1 us -> 80.1 us (0.976)
  Pallas kernels: 78.1 us -> 76.1 us
    pallas_call x1, Pallas kernels: 78.1 us -> 76.1 us  [shards(): pl.pallas_call(kernel, out_shape=(jax.ShapeDtypeStruct((8, 2, 64, 64), F3...]
where the time goes in v4:
time: 80.1 us; the launch traced here: 80 us
  Pallas kernels  76.1 us (95%)
  local copies, waits for them, and re-layouts  2.58 us (3%)
  between operations  1.29 us (2%)
    pallas_call x1, Pallas kernels, shards(): pl.pallas_call(kernel, out_shape=(jax.ShapeDtypeStruct((8, 2, 64, 64), F3...  76.1 us
    unnamed x4, local copies, waits for them, and re-layouts  2.58 us

profile of v4, /device:TPU:1, one launch (start us, length us, event | category | flops | bytes accessed | tf_op | source)
XLA Modules:
  0.0 80.0 jit_solution(10768526734033317719)
XLA Ops:
  1.3 76.1 %shard_map.86 = (f32[8,2,64,64]{3,2,1,0:T(8,128)}, f32[2,2,64,64]{3,2,1,0:T(8,128)}) custom-call(f32[32,64,64]{2,1,0:T(8,128)} %bitcast.6, s32[1,32]{1,0:T(1,128)} %bitcast.8, s32[1,32]{1,0:T(1,128)} %bitcast.9, s32[1,1]{1,0:T(1,128)S(6)} %copy.11.count_ref, f32[8,64,64]{2,1,0:T(8,128)} %bitcast.7, s32[1,8]{1,0:T(1,128)} %bitcast.10, s32[1,8]{1,0:T(1,128)} %bitcast.11), custom_call_target="tpu_custom_call" | custom-call | tf_op jit(solution)/shard_map/pallas_call | solution.py:515
  77.4 0.0 copy-start
  77.4 1.9 %copy.12 = f32[8,2,64,64]{3,2,1,0:T(8,128)} copy(f32[8,2,64,64]{3,2,1,0:T(8,128)} %get-tuple-element.4) | data formatting | bytes 524288
  79.4 0.0 copy-done
  79.4 0.7 copy.13
Async XLA Ops:
  77.4 1.9 %copy-start = (f32[2,2,64,64]{3,2,1,0:T(8,128)S(1)}, f32[2,2,64,64]{3,2,1,0:T(8,128)}, u32[]{:S(2)}) copy-start(f32[2,2,64,64]{3,2,1,0:T(8,128)} %get-tuple-element.5) | copy-start | bytes 196612

commit v5 on v4

--- a/solution.py
+++ b/solution.py
@@ -151,14 +151,12 @@
         hot = (which[pl.ds(0, 1), pl.ds(0, 2 * LA)] == place).astype(F32).astype(BF16)
 
         def row(step, carry):
-            rho = n * 8 + step * 2
-            h0, l0 = split(src[rho])
-            h1, l1 = split(src[rho + 1])
-            both = jnp.concatenate(
-                [jnp.concatenate([h0, l0], axis=0), jnp.concatenate([h1, l1], axis=0)], axis=1
-            )
-            tiles = dot(hot, both)
-            for e in range(2):
+            rho = n * 8 + step * 4
+            columns = []
+            for e in range(4):
+                columns.append(jnp.concatenate(split(src[rho + e]), axis=0))
+            tiles = dot(hot, jnp.concatenate(columns, axis=1))
+            for e in range(4):
                 t = tiles[:, e * 128 : e * 128 + 128]
                 for m in range(4):
                     even, odd = t[m * 16 : m * 16 + 8], t[m * 16 + 8 : m * 16 + 16]
@@ -170,7 +168,7 @@
                     alo[at, at_rows, pl.ds(m * 128, 128)] = lo
             return carry
 
-        lax.fori_loop(0, 4, row, 0)
+        lax.fori_loop(0, 2, row, 0, unroll=2)
 
     def dense(ref, b, s, k):
         tile = ref[b, s, pl.ds(k * 32, 32), :]

time: 80.1 us -> 78.4 us (0.979)
  Pallas kernels: 76.1 us -> 73.7 us
    pallas_call x1, Pallas kernels: 76.1 us -> 73.7 us  [shards(): pl.pallas_call(kernel, out_shape=(jax.ShapeDtypeStruct((8, 2, 64, 64), F3...]
where the time goes in v5:
time: 78.4 us; the launch traced here: 77.5 us
  Pallas kernels  73.7 us (94%)
  local copies, waits for them, and re-layouts  2.58 us (3%)
  between operations  1.29 us (2%)
    pallas_call x1, Pallas kernels, shards(): pl.pallas_call(kernel, out_shape=(jax.ShapeDtypeStruct((8, 2, 64, 64), F3...  73.7 us
    unnamed x4, local copies, waits for them, and re-layouts  2.58 us

profile of v5, /device:TPU:1, one launch (start us, length us, event | category | flops | bytes accessed | tf_op | source)
XLA Modules:
  0.0 77.5 jit_solution(14180443895512942696)
XLA Ops:
  1.3 73.7 %shard_map.86 = (f32[8,2,64,64]{3,2,1,0:T(8,128)}, f32[2,2,64,64]{3,2,1,0:T(8,128)}) custom-call(f32[32,64,64]{2,1,0:T(8,128)} %bitcast.6, s32[1,32]{1,0:T(1,128)} %bitcast.8, s32[1,32]{1,0:T(1,128)} %bitcast.9, s32[1,1]{1,0:T(1,128)S(6)} %copy.11.count_ref, f32[8,64,64]{2,1,0:T(8,128)} %bitcast.7, s32[1,8]{1,0:T(1,128)} %bitcast.10, s32[1,8]{1,0:T(1,128)} %bitcast.11), custom_call_target="tpu_custom_call" | custom-call | tf_op jit(solution)/shard_map/pallas_call | solution.py:513
  74.9 0.0 copy-start
  74.9 1.9 %copy.12 = f32[8,2,64,64]{3,2,1,0:T(8,128)} copy(f32[8,2,64,64]{3,2,1,0:T(8,128)} %get-tuple-element.4) | data formatting | bytes 524288
  76.9 0.0 copy-done
  76.9 0.7 copy.13
Async XLA Ops:
  74.9 1.9 %copy-start = (f32[2,2,64,64]{3,2,1,0:T(8,128)S(1)}, f32[2,2,64,64]{3,2,1,0:T(8,128)}, u32[]{:S(2)}) copy-start(f32[2,2,64,64]{3,2,1,0:T(8,128)} %get-tuple-element.5) | copy-start | bytes 196612

commit v6 on v5

--- a/solution.py
+++ b/solution.py
@@ -12,7 +12,7 @@
 UR = 264
 UH = 136
 LA = 32
-HALF = ((0, 256), (256, 256))
+ORDER = ((1, 0, 3, 2), (0, 1, 2, 3))
 PART = (pl.ds(0, UH), pl.ds(UH, UR - UH))
 
 M_ID = 0
@@ -24,10 +24,12 @@
 Z_ID = 29
 PY_ID = 37
 RS_ID = 45
-CC_ID = 61
-CX_ID = 65
-CY_ID = 73
-N_ID = 75
+CC_ID = 77
+CX_ID = 85
+CY_ID = 93
+H_ID = 95
+F_ID = 96
+N_ID = 97
 
 
 def split(v):
@@ -42,7 +44,7 @@
 def kernel(
     op_hbm, rows_ref, cols_ref, count_ref, pro_ref, pcols_ref, plive_ref,
     prod_hbm, coarse_ref,
-    op_ref, prod_ref, meta, mnear,
+    op_ref, prod_ref, meta, mnear, hop,
     unit, alist, anear, panel, pror, ahi, alo, rhi, rlo, q, rsr, rsl, pthi, ptlo, pcat,
     cpart, crecv, xr0, xl0, xr1, xl1, yrecv,
     ssem, rsem, lsem,
@@ -66,6 +68,18 @@
     across = rowdev(yh, lax.rem(z + x + 2 * core, 4), z // 4)[0], yl * 8 + plane
     source = rowdev(yh, z // 2, lax.rem(z, 2))[0], yl * 8 + s0
     own_across = jnp.logical_and(s0 == z, plane == z)
+    via_x, via_src_x = lax.rem(z + x + 2 * core, 4), lax.rem(x + 12 - z - 2 * core, 4)
+    via, via_src = rowdev(yh, via_x, core), rowdev(yh, via_src_x, core)
+    via_self = via_x == x
+    via_last = jnp.logical_and(plane == z, z // 4 == core)
+    fwd_plane = 2 * via_src_x + core
+    fwd = rowdev(yh, x, z // 4)[0], yl * 8 + fwd_plane
+    fwd_src = rowdev(yh, x, lax.rem(z, 2))[0], yl * 8 + s0
+    fwd_self = jnp.logical_and(fwd_plane == z, z // 4 == core)
+    direct = jnp.logical_and(via_self, jnp.logical_not(own_across))
+    final_hop = jnp.logical_and(jnp.logical_not(via_self), via_last)
+    first_hop = jnp.logical_not(jnp.logical_or(via_self, via_last))
+    serves = jnp.logical_not(jnp.logical_or(via_self, fwd_self))
 
     def send(src, dst, k, dev):
         pltpu.make_async_remote_copy(
@@ -93,12 +107,25 @@
         pl.semaphore_signal(barrier, inc=1, device_id=across, device_id_type=MESH)
         pl.semaphore_signal(barrier, inc=1, device_id=source, device_id_type=MESH)
 
+    @pl.when(jnp.logical_not(via_self))
+    def _():
+        pl.semaphore_signal(barrier, inc=1, device_id=via, device_id_type=MESH)
+        pl.semaphore_signal(barrier, inc=1, device_id=via_src, device_id_type=MESH)
+
+    @pl.when(jnp.logical_not(fwd_self))
+    def _():
+        pl.semaphore_signal(barrier, inc=1, device_id=fwd, device_id_type=MESH)
+        pl.semaphore_signal(barrier, inc=1, device_id=fwd_src, device_id_type=MESH)
+
     for k in range(8):
         live = plive_ref[0, k].astype(F32)
         unit[pl.ds(k * 32, 32), :] = pack(pro_ref[k]) * live
         unit[pl.ds(256 + k, 1), :] = jnp.full((1, 128), pcols_ref[0, k].astype(F32))
 
-    pl.semaphore_wait(barrier, jnp.where(own_across, 7, 9))
+    pl.semaphore_wait(
+        barrier,
+        7 + jnp.where(own_across, 0, 2) + jnp.where(via_self, 0, 2) + jnp.where(fwd_self, 0, 2),
+    )
 
     @pl.when(own_across)
     def _():
@@ -106,8 +133,19 @@
 
     @pl.when(jnp.logical_not(own_across))
     def _():
-        for p in range(2):
-            send(unit.at[PART[p]], panel.at[yh, z].at[PART[p]], T_ID + p, across)
+        send(unit.at[PART[0]], panel.at[yh, z].at[PART[0]], T_ID, across)
+
+    @pl.when(direct)
+    def _():
+        send(unit.at[PART[1]], panel.at[yh, z].at[PART[1]], T_ID + 1, across)
+
+    @pl.when(final_hop)
+    def _():
+        send(unit.at[PART[1]], panel.at[yh, z].at[PART[1]], T_ID + 1, via)
+
+    @pl.when(first_hop)
+    def _():
+        send(unit.at[PART[1]], hop, H_ID, via)
 
     keep = pltpu.make_async_copy(unit, pror.at[yl, z], lsem.at[1])
     keep.start()
@@ -180,9 +218,19 @@
         return top, bot
 
     zu = pror.at[yl, z]
-    send(unit, zu, Z_ID, zright)
-    send(unit, zu, Z_ID + 4, zleft)
     build_a(alist, meta, yl, 0)
+
+    @pl.when(serves)
+    def _():
+        arrived(hop, H_ID)
+        pltpu.make_async_remote_copy(
+            src_ref=hop,
+            dst_ref=panel.at[yh, z].at[PART[1]],
+            send_sem=ssem.at[F_ID],
+            recv_sem=rsem.at[T_ID + 1],
+            device_id=fwd,
+            device_id_type=MESH,
+        ).start()
 
     def ring(off):
         return 4 * core + lax.rem(x + turn + off, 4)
@@ -248,8 +296,9 @@
     send_piece(3)
     send(u, u, CORE_ID, other)
     keep.wait()
+    send(unit, zu, Z_ID, zright)
+    send(unit, zu, Z_ID + 4, zleft)
     send(zu, zu, PY_ID, ynear)
-    zstep(1)
     build_a(alist, meta, yl, 1)
     onward(mine, X_ID)
     build_a(alist, meta, yl, 2)
@@ -258,17 +307,17 @@
         arrived(u.at[PART[p]], Y_ID + p)
         spread(theirs, X_ID + 6, p)
     send(u, u, CORE_ID + 4, other)
+    zstep(1)
     beside(mine, X_ID, CORE_ID)
     build_a(alist, meta, yl, 3)
-    zstep(2)
     onward(theirs, X_ID + 6)
     far(mine, X_ID, CORE_ID)
+    zstep(2)
     arrived(mnear, M_ID)
     for n in range(2):
         arrived(anear.at[pl.ds(n * 8, 8)], A_ID + n)
         build_a(anear, mnear, 1 - yl, n)
     beside(theirs, X_ID + 6, CORE_ID + 4)
-    zstep(3)
     far(theirs, X_ID + 6, CORE_ID + 4)
     for n in range(2, 4):
         arrived(anear.at[pl.ds(n * 8, 8)], A_ID + n)
@@ -290,50 +339,42 @@
 
         lax.fori_loop(0, 2, block, 0)
 
-    def chunk_one(d):
-        build_r(d, 0)
-
-        def part(m, carry):
-            rows = pl.ds(pl.multiple_of(m * 256, 256), 256)
-            acc = jnp.zeros((256, 128), F32)
+    left128 = lax.broadcasted_iota(jnp.int32, (128, 128), 1) < 64
+    left64 = lax.broadcasted_iota(jnp.int32, (64, 128), 1) < 64
+
+    def chunk(*ds):
+        wide = 128 * len(ds)
+        for at, d in enumerate(ds):
+            build_r(d, at)
+
+        def part(e, carry):
+            acc = jnp.zeros((256, wide), F32)
+            top = pl.ds(pl.multiple_of(e * 128, 128), 128)
+            bot = pl.ds(pl.multiple_of(256 + e * 128, 128), 128)
             for b in range(2):
-                h, l = ahi[b, rows, :], alo[b, rows, :]
-                rh = rhi[b, :, pl.ds(0, 128)]
-                acc = acc + dot(h, rh) + dot(h, rlo[b, :, pl.ds(0, 128)]) + dot(l, rh)
-            q[d, rows, :] = acc
+                h = jnp.concatenate([ahi[b, top, :], ahi[b, bot, :]], axis=0)
+                l = jnp.concatenate([alo[b, top, :], alo[b, bot, :]], axis=0)
+                rh = rhi[b, :, pl.ds(0, wide)]
+                acc = acc + dot(h, rh) + dot(h, rlo[b, :, pl.ds(0, wide)]) + dot(l, rh)
+            for at, d in enumerate(ds):
+                t, u = acc[:128, at * 128 : at * 128 + 128], acc[128:, at * 128 : at * 128 + 128]
+                q[d, e] = jnp.where(left128, t, pltpu.roll(u, 64, 1))
+                q[d, 2 + e] = jnp.where(left128, pltpu.roll(t, 64, 1), u)
             return carry
 
         lax.fori_loop(0, 2, part, 0)
 
-    def chunk(d0, d1):
-        build_r(d0, 0)
-        build_r(d1, 1)
-
-        def part(m, carry):
-            rows = pl.ds(pl.multiple_of(m * 256, 256), 256)
-            acc = jnp.zeros((256, 256), F32)
-            for b in range(2):
-                h, l = ahi[b, rows, :], alo[b, rows, :]
-                acc = acc + dot(h, rhi[b]) + dot(h, rlo[b]) + dot(l, rhi[b])
-            q[d0, rows, :] = acc[:, :128]
-            q[d1, rows, :] = acc[:, 128:]
-            return carry
-
-        lax.fori_loop(0, 2, part, 0)
-
-    def rs_id(step, half, way):
-        return RS_ID + (step * 2 + half) * 2 + way
-
-    def rs_send(d, step, half, way):
-        rows = pl.ds(*HALF[half])
+    def rs_id(step, blk, way):
+        return RS_ID + (step * 4 + blk) * 2 + way
+
+    def rs_send(d, step, blk, way):
         buf = (rsr, rsl)[way]
-        send(q.at[d, rows], buf.at[step, rows], rs_id(step, half, way), (zright, zleft)[way])
-
-    def rs_add(d, step, half, way):
-        rows = pl.ds(*HALF[half])
+        send(q.at[d, blk], buf.at[step, blk], rs_id(step, blk, way), (zright, zleft)[way])
+
+    def rs_add(d, step, blk, way):
         buf = (rsr, rsl)[way]
-        arrived(buf.at[step, rows], rs_id(step, half, way))
-        q[d, rows, :] = q[d, rows, :] + buf[step, rows, :]
+        arrived(buf.at[step, blk], rs_id(step, blk, way))
+        q[d, blk] = q[d, blk] + buf[step, blk]
 
     def build_t(b, s):
         flag = pror[b, s, pl.ds(256, 8), :]
@@ -350,127 +391,150 @@
             pthi[lax.rem(g, 2), lax.rem(g // 2, 4), rows, pl.ds(m * 128, 128)] = hi
             ptlo[lax.rem(g, 2), lax.rem(g // 2, 4), rows, pl.ds(m * 128, 128)] = lo
 
-    chunk_one(4)
-    rs_send(4, 0, 0, 0)
-    rs_send(4, 0, 1, 1)
+    def own_t(s, carry):
+        build_t(yl, s)
+        return carry
+
+    def pass_step(step):
+        for n in range(4):
+            for way, d in ((0, 4 - step), (1, 4 + step)):
+                blk = ORDER[way][n]
+                if step > 1 or blk % 2 == way:
+                    rs_add(d, step - 1, blk, way)
+                rs_send(d, step, blk, way)
+
+    zstep(3)
+    chunk(4)
+    for blk in range(4):
+        rs_send(4, 0, blk, blk % 2)
     chunk(3, 5)
-    rs_send(3, 1, 1, 0)
-    rs_send(5, 1, 0, 1)
-    rs_add(3, 0, 0, 0)
-    rs_send(3, 1, 0, 0)
-    rs_add(5, 0, 1, 1)
-    rs_send(5, 1, 1, 1)
+    pass_step(1)
     zfar = pror.at[yl, lax.rem(z + 4, 8)]
     arrived(zfar.at[PART[0]], Z_ID + 3)
     arrived(zfar.at[PART[1]], Z_ID + 7)
     send(zfar, zfar, PY_ID + 7, ynear)
-
     chunk(2, 6)
-
-    for half_r, half_l in ((1, 0), (0, 1)):
-        rs_add(2, 1, half_r, 0)
-        rs_send(2, 2, half_r, 0)
-        rs_add(6, 1, half_l, 1)
-        rs_send(6, 2, half_l, 1)
+    lax.fori_loop(0, 8, own_t, 0)
+    pass_step(2)
     chunk(1, 7)
-
-    def own_t(s, carry):
-        build_t(yl, s)
-        return carry
-
-    for half_r, half_l in ((1, 0), (0, 1)):
-        rs_add(1, 2, half_r, 0)
-        rs_send(1, 3, half_r, 0)
-        rs_add(7, 2, half_l, 1)
-        rs_send(7, 3, half_l, 1)
-    chunk_one(0)
-    lax.fori_loop(0, 8, own_t, 0)
-
-    near = [pror.at[1 - yl, z]]
+    chunk(0)
+    pass_step(3)
+
+    near = [z]
     for step in (1, 2, 3):
-        near += [pror.at[1 - yl, lax.rem(z + 8 - step, 8)], pror.at[1 - yl, lax.rem(z + step, 8)]]
-    near.append(pror.at[1 - yl, lax.rem(z + 4, 8)])
-    for n, ref in enumerate(near):
-        arrived(ref, PY_ID + n)
-
-    def near_t(s, carry):
-        build_t(1 - yl, s)
-        return carry
-
-    lax.fori_loop(0, 8, near_t, 0)
-
-    for half in (0, 1):
-        rs_add(0, 3, half, 0)
-        rs_add(0, 3, half, 1)
-        rows = pl.ds(*HALF[half])
-        hi, lo = split(q[0, rows, :])
-        pcat[rows, pl.ds(0, 128)] = hi
-        pcat[rows, pl.ds(128, 128)] = lo
-
-    def coarse_part(gc, gx):
-        v = dot(pthi[gc, gx], pcat[...])
-        v = v[:, :128] + v[:, 128:] + dot(ptlo[gc, gx], pcat[:, :128])
-        cpart[gc, gx, 0] = v[:128]
-        cpart[gc, gx, 1] = v[128:]
-
-    def to_other(gx, n):
-        coarse_part(1 - core, gx)
-        send(cpart.at[1 - core, gx], crecv.at[gx], CC_ID + n, other)
-
-    def from_core(gx, n):
-        coarse_part(core, gx)
-        arrived(crecv.at[gx], CC_ID + n)
-        cpart[core, gx] = cpart[core, gx] + crecv[gx]
+        near += [lax.rem(z + 8 - step, 8), lax.rem(z + step, 8)]
+    near.append(lax.rem(z + 4, 8))
+    for n, shard in enumerate(near):
+        arrived(pror.at[1 - yl, shard], PY_ID + n)
+        build_t(1 - yl, shard)
+
+    def finish(m):
+        for e in range(2):
+            for way in (0, 1):
+                rs_add(0, 3, 2 * m + e, way)
+            v = q[0, 2 * m + e]
+            hi = v.astype(BF16).astype(F32)
+            lo = v - hi
+            pcat[m, pl.ds(e * 128, 128), :] = jnp.where(left128, hi, pltpu.roll(lo, 64, 1)).astype(BF16)
+            pcat[m, pl.ds(256 + e * 128, 128), :] = jnp.where(left128, pltpu.roll(hi, 64, 1), lo).astype(BF16)
+
+    def coarse_part(gc, gx, m):
+        a = dot(pthi[gc, gx], pcat[m])
+        v = a + pltpu.roll(a, 64, 1) + dot(ptlo[gc, gx], pcat[m])
+        for gy in range(2):
+            top, bot = v[gy * 128 : gy * 128 + 64], v[gy * 128 + 64 : gy * 128 + 128]
+            cpart[gc, gx, m, gy] = jnp.where(left64, top, pltpu.roll(bot, 64, 1))
+
+    def to_other(gx, m, n):
+        coarse_part(1 - core, gx, m)
+        send(cpart.at[1 - core, gx, m], crecv.at[gx, m], CC_ID + 4 * m + n, other)
+
+    def from_core(gx, m, n):
+        coarse_part(core, gx, m)
+        arrived(crecv.at[gx, m], CC_ID + 4 * m + n)
+        cpart[core, gx, m] = cpart[core, gx, m] + crecv[gx, m]
 
     x2 = lax.rem(x + 2, 4)
     xp, xm = lax.rem(x + 1, 4), lax.rem(x + 3, 4)
     cp = cpart.at[core]
-    to_other(x2, 0)
-    to_other(xp, 1)
-    from_core(x2, 0)
-    top_bot = (pl.ds(0, 64), pl.ds(64, 64))
-    for h, rows in enumerate(top_bot):
-        send(cp.at[x2, 0, rows], xr0.at[rows], CX_ID + h, xright)
-        send(cp.at[x2, 1, rows], xl0.at[rows], CX_ID + 2 + h, xleft)
-    to_other(xm, 2)
-    from_core(xp, 1)
-    to_other(x, 3)
-    from_core(xm, 2)
-    for h, rows in enumerate(top_bot):
-        arrived(xr0.at[rows], CX_ID + h)
-        cpart[core, xp, 0, rows] = cpart[core, xp, 0, rows] + xr0[rows]
-        send(cp.at[xp, :, rows], xr1.at[:, rows], CX_ID + 4 + h, xright)
-        arrived(xl0.at[rows], CX_ID + 2 + h)
-        cpart[core, xm, 1, rows] = cpart[core, xm, 1, rows] + xl0[rows]
-        send(cp.at[xm, :, rows], xl1.at[:, rows], CX_ID + 6 + h, xleft)
-    from_core(x, 3)
+
+    def first(m):
+        to_other(x2, m, 0)
+        to_other(xp, m, 1)
+        from_core(x2, m, 0)
+        send(cp.at[x2, m, 0], xr0.at[m], CX_ID + 4 * m, xright)
+        send(cp.at[x2, m, 1], xl0.at[m], CX_ID + 4 * m + 1, xleft)
+
+    def sides(m):
+        to_other(xm, m, 2)
+        from_core(xp, m, 1)
+        from_core(xm, m, 2)
+
+    def second(m):
+        arrived(xr0.at[m], CX_ID + 4 * m)
+        cpart[core, xp, m, 0] = cpart[core, xp, m, 0] + xr0[m]
+        send(cp.at[xp, m], xr1.at[m], CX_ID + 4 * m + 2, xright)
+        arrived(xl0.at[m], CX_ID + 4 * m + 1)
+        cpart[core, xm, m, 1] = cpart[core, xm, m, 1] + xl0[m]
+        send(cp.at[xm, m], xl1.at[m], CX_ID + 4 * m + 3, xleft)
+
+    def third(m):
+        arrived(xr1.at[m], CX_ID + 4 * m + 2)
+        arrived(xl1.at[m], CX_ID + 4 * m + 3)
+        cpart[core, x, m, 1 - yh] = cpart[core, x, m, 1 - yh] + xr1[m, 1 - yh] + xl1[m, 1 - yh]
+        send(cp.at[x, m, 1 - yh], yrecv.at[m], CY_ID + m, yfar)
+
+    finish(0)
+    first(0)
+    finish(1)
+    first(1)
+    sides(0)
+    second(0)
+    sides(1)
+    second(1)
+    to_other(x, 0, 3)
+    to_other(x, 1, 3)
+    from_core(x, 0, 3)
+    third(0)
+    from_core(x, 1, 3)
     for i in range(8):
         for h in range(2):
-            v = q[0, pl.ds(h * 8 + i, 32, stride=16), :]
-            prod_ref[i, 0, pl.ds(h * 32, 32), :] = v[:, :64]
-            prod_ref[i, 1, pl.ds(h * 32, 32), :] = v[:, 64:]
+            for m in range(2):
+                for e in range(2):
+                    v = q[0, 2 * m + e, pl.ds(h * 8 + i, 8, stride=16), :]
+                    prod_ref[i, m, pl.ds(h * 32 + e * 8, 8), :] = v[:, :64]
+                    prod_ref[i, m, pl.ds(h * 32 + 16 + e * 8, 8), :] = v[:, 64:]
     put = pltpu.make_async_copy(prod_ref, prod_hbm, lsem.at[3])
     put.start()
-    for h, rows in enumerate(top_bot):
-        arrived(xr1.at[:, rows], CX_ID + 4 + h)
-        arrived(xl1.at[:, rows], CX_ID + 6 + h)
-        cpart[core, x, 1 - yh, rows] = cpart[core, x, 1 - yh, rows] + xr1[1 - yh, rows] + xl1[1 - yh, rows]
-        send(cp.at[x, 1 - yh, rows], yrecv.at[rows], CY_ID + h, yfar)
-    for h, rows in enumerate(top_bot):
-        total = cpart[core, x, yh, rows] + xr1[yh, rows] + xl1[yh, rows]
-        arrived(yrecv.at[rows], CY_ID + h)
-        total = total + yrecv[rows]
-        for b in range(2):
-            coarse_ref[h, b] = total[:, b * 64 : b * 64 + 64]
+    third(1)
+    for m in range(2):
+        total = cpart[core, x, m, yh] + xr1[m, yh] + xl1[m, yh]
+        arrived(yrecv.at[m], CY_ID + m)
+        total = total + yrecv[m]
+        coarse_ref[0, m] = total[:, :64]
+        coarse_ref[1, m] = total[:, 64:]
 
     u = panel.at[0, 0]
+
+    @pl.when(jnp.logical_not(own_across))
+    def _():
+        sent(u.at[PART[0]], T_ID)
+
+    @pl.when(jnp.logical_or(direct, final_hop))
+    def _():
+        sent(u.at[PART[1]], T_ID + 1)
+
+    @pl.when(first_hop)
+    def _():
+        sent(hop, H_ID)
+
+    @pl.when(serves)
+    def _():
+        sent(hop, F_ID)
+
     zu = pror.at[0, 0]
     for p in range(2):
         part = u.at[PART[p]]
-
-        @pl.when(jnp.logical_not(own_across))
-        def _():
-            sent(part, T_ID + p)
 
         sent(part, Y_ID + p)
         for k in (X_ID, X_ID + 6):
@@ -489,21 +553,20 @@
         sent(zu, Z_ID + 4 + n)
     sent(zu.at[PART[0]], Z_ID + 3)
     sent(zu.at[PART[1]], Z_ID + 7)
-    piece = q.at[0, pl.ds(0, 256)]
-    sent(piece, rs_id(0, 0, 0))
-    sent(piece, rs_id(0, 1, 1))
-    for step in (1, 2, 3):
-        for half in (0, 1):
+    piece = q.at[0, 0]
+    for blk in range(4):
+        sent(piece, rs_id(0, blk, blk % 2))
+        for step in (1, 2, 3):
             for way in (0, 1):
-                sent(piece, rs_id(step, half, way))
-    for n in range(4):
-        sent(crecv.at[0], CC_ID + n)
-    for h, rows in enumerate(top_bot):
-        sent(xr0.at[rows], CX_ID + h)
-        sent(xl0.at[rows], CX_ID + 2 + h)
-        sent(xr1.at[:, rows], CX_ID + 4 + h)
-        sent(xl1.at[:, rows], CX_ID + 6 + h)
-        sent(yrecv.at[rows], CY_ID + h)
+                sent(piece, rs_id(step, blk, way))
+    for n in range(8):
+        sent(crecv.at[0, 0], CC_ID + n)
+    for m in range(2):
+        sent(xr0.at[m], CX_ID + 4 * m)
+        sent(xl0.at[m], CX_ID + 4 * m + 1)
+        sent(xr1.at[m], CX_ID + 4 * m + 2)
+        sent(xl1.at[m], CX_ID + 4 * m + 3)
+        sent(yrecv.at[m], CY_ID + m)
 
 
 def shards(op_tiles, op_rows, op_cols, op_count, pro_tiles, pro_cols, pro_live):
@@ -523,6 +586,7 @@
             pltpu.VMEM((8, 2, 64, 64), F32),
             pltpu.VMEM((8, 128), F32),
             pltpu.VMEM((8, 128), F32),
+            pltpu.VMEM((UR - UH, 128), F32),
             pltpu.VMEM((UR, 128), F32),
             pltpu.VMEM((32, LA, 128), F32),
             pltpu.VMEM((32, LA, 128), F32),
@@ -532,19 +596,19 @@
             pltpu.VMEM((2, 512, 512), BF16),
             pltpu.VMEM((2, 512, 256), BF16),
             pltpu.VMEM((2, 512, 256), BF16),
-            pltpu.VMEM((8, 512, 128), F32),
-            pltpu.VMEM((4, 512, 128), F32),
-            pltpu.VMEM((4, 512, 128), F32),
+            pltpu.VMEM((8, 4, 128, 128), F32),
+            pltpu.VMEM((4, 4, 128, 128), F32),
+            pltpu.VMEM((4, 4, 128, 128), F32),
             pltpu.VMEM((2, 4, 256, 512), BF16),
             pltpu.VMEM((2, 4, 256, 512), BF16),
-            pltpu.VMEM((512, 256), BF16),
-            pltpu.VMEM((2, 4, 2, 128, 128), F32),
-            pltpu.VMEM((4, 2, 128, 128), F32),
-            pltpu.VMEM((128, 128), F32),
-            pltpu.VMEM((128, 128), F32),
-            pltpu.VMEM((2, 128, 128), F32),
-            pltpu.VMEM((2, 128, 128), F32),
-            pltpu.VMEM((128, 128), F32),
+            pltpu.VMEM((2, 512, 128), BF16),
+            pltpu.VMEM((2, 4, 2, 2, 64, 128), F32),
+            pltpu.VMEM((4, 2, 2, 64, 128), F32),
+            pltpu.VMEM((2, 64, 128), F32),
+            pltpu.VMEM((2, 64, 128), F32),
+            pltpu.VMEM((2, 2, 64, 128), F32),
+            pltpu.VMEM((2, 2, 64, 128), F32),
+            pltpu.VMEM((2, 64, 128), F32),
             pltpu.SemaphoreType.DMA((N_ID,)),
             pltpu.SemaphoreType.DMA((N_ID,)),
             pltpu.SemaphoreType.DMA((4,)),

time: 78.4 us -> 77 us (0.982); the launches traced: 77.5 us -> 76.9 us
  no operation moved by 1% of the time
where the time goes in v6:
time: 77 us; the launch traced here: 76.9 us
  Pallas kernels  73 us (95%)
  local copies, waits for them, and re-layouts  2.58 us (3%)
  between operations  1.29 us (2%)
    pallas_call x1, Pallas kernels, shards(): pl.pallas_call(kernel, out_shape=(jax.ShapeDtypeStruct((8, 2, 64, 64), F3...  73 us
    unnamed x4, local copies, waits for them, and re-layouts  2.58 us

profile of v6, /device:TPU:1, one launch (start us, length us, event | category | flops | bytes accessed | tf_op | source)
XLA Modules:
  0.0 76.9 jit_solution(18298597909187008598)
XLA Ops:
  1.3 73.0 %shard_map.86 = (f32[8,2,64,64]{3,2,1,0:T(8,128)}, f32[2,2,64,64]{3,2,1,0:T(8,128)}) custom-call(f32[32,64,64]{2,1,0:T(8,128)} %bitcast.6, s32[1,32]{1,0:T(1,128)} %bitcast.8, s32[1,32]{1,0:T(1,128)} %bitcast.9, s32[1,1]{1,0:T(1,128)S(6)} %copy.11.count_ref, f32[8,64,64]{2,1,0:T(8,128)} %bitcast.7, s32[1,8]{1,0:T(1,128)} %bitcast.10, s32[1,8]{1,0:T(1,128)} %bitcast.11), custom_call_target="tpu_custom_call" | custom-call | tf_op jit(solution)/shard_map/pallas_call | solution.py:576
  74.3 0.0 copy-start
  74.3 1.9 %copy.12 = f32[8,2,64,64]{3,2,1,0:T(8,128)} copy(f32[8,2,64,64]{3,2,1,0:T(8,128)} %get-tuple-element.4) | data formatting | bytes 524288
  76.3 0.0 copy-done
  76.3 0.7 copy.13
Async XLA Ops:
  74.3 1.9 %copy-start = (f32[2,2,64,64]{3,2,1,0:T(8,128)S(1)}, f32[2,2,64,64]{3,2,1,0:T(8,128)}, u32[]{:S(2)}) copy-start(f32[2,2,64,64]{3,2,1,0:T(8,128)} %get-tuple-element.5) | copy-start | bytes 196612

commit v7 on v6

--- a/solution.py
+++ b/solution.py
@@ -417,8 +417,8 @@
     lax.fori_loop(0, 8, own_t, 0)
     pass_step(2)
     chunk(1, 7)
+    pass_step(3)
     chunk(0)
-    pass_step(3)
 
     near = [z]
     for step in (1, 2, 3):

time: 77 us -> 77.4 us (level)
  no operation moved by 1% of the time
where the time goes in v7:
time: 77.4 us; the launch traced here: 77.3 us
  Pallas kernels  73.4 us (95%)
  local copies, waits for them, and re-layouts  2.58 us (3%)
  between operations  1.29 us (2%)
    pallas_call x1, Pallas kernels, shards(): pl.pallas_call(kernel, out_shape=(jax.ShapeDtypeStruct((8, 2, 64, 64), F3...  73.4 us
    unnamed x4, local copies, waits for them, and re-layouts  2.58 us

profile of v7, /device:TPU:1, one launch (start us, length us, event | category | flops | bytes accessed | tf_op | source)
XLA Modules:
  0.0 77.3 jit_solution(1772782453897846917)
XLA Ops:
  1.3 73.4 %shard_map.86 = (f32[8,2,64,64]{3,2,1,0:T(8,128)}, f32[2,2,64,64]{3,2,1,0:T(8,128)}) custom-call(f32[32,64,64]{2,1,0:T(8,128)} %bitcast.6, s32[1,32]{1,0:T(1,128)} %bitcast.8, s32[1,32]{1,0:T(1,128)} %bitcast.9, s32[1,1]{1,0:T(1,128)S(6)} %copy.11.count_ref, f32[8,64,64]{2,1,0:T(8,128)} %bitcast.7, s32[1,8]{1,0:T(1,128)} %bitcast.10, s32[1,8]{1,0:T(1,128)} %bitcast.11), custom_call_target="tpu_custom_call" | custom-call | tf_op jit(solution)/shard_map/pallas_call | solution.py:576
  74.7 0.0 copy-start
  74.7 1.9 %copy.12 = f32[8,2,64,64]{3,2,1,0:T(8,128)} copy(f32[8,2,64,64]{3,2,1,0:T(8,128)} %get-tuple-element.4) | data formatting | bytes 524288
  76.7 0.0 copy-done
  76.7 0.7 copy.13
Async XLA Ops:
  74.7 1.9 %copy-start = (f32[2,2,64,64]{3,2,1,0:T(8,128)S(1)}, f32[2,2,64,64]{3,2,1,0:T(8,128)}, u32[]{:S(2)}) copy-start(f32[2,2,64,64]{3,2,1,0:T(8,128)} %get-tuple-element.5) | copy-start | bytes 196612
